TPU v7x, 32 devices: a whole 2x2x4 slice. The times are simulated.
32 devices in a mesh: lat: 2 (over x), lon: 4 (over y, core), lev: 4 (over z).
Axes of the slice: x: 2, y: 2, z: 4, core: 2. Of those that a mesh axis runs over, the one named last changes fastest.
Arguments:
- adj_final: float32 [2, 72, 32, 512], P(None, 'lev', 'lat', 'lon'), may hold values from -6 to 6
- stencil: float32 [5, 72, 32, 512], P(None, 'lev', 'lat', 'lon'), may hold values from -0.3 to 0.3
- landmask: int32 [72, 32, 512], P('lev', 'lat', 'lon'), may hold values 0 or 1
- thickness: float32 [72, 32, 512], P(None, ('lat', 'lev'), 'lon'), may hold values from 0.5 to 2
- diffusivity: float32 [72, 32, 512], P(None, ('lat', 'lev'), 'lon'), may hold values from 0.05 to 5
- level_counts: int32 [32, 512], P(('lat', 'lev'), 'lon'), may hold values from 36 to 72
- fold_partner: int32 [512], P('lon'), may hold values from 0 to 511, as said below
Outputs:
- adj_start: float32 [2, 72, 32, 512], P(None, 'lev', 'lat', 'lon')
Inputs may be any that keep to these rules, and one draw needn't show every extreme that they name: `fold_partner`: A column i in block b = i // 128 of 128 columns has its partner in block 3 - b; within a block the partners are all different.
All inputs are finite; a program needn't handle non-finite values. No bound on the sum of `landmask` on one device may be relied on, other than what follows from the above.
Results may differ from a plain program's by a relative error of at most 0.0001.
Values sent between devices are 32-bit elements; how exact they have to be, the bound alone decides.
No kernel may reach another device: no remote copies, remote signals or barrier semaphores. Data moves between devices by JAX's collectives and lax.ppermute only.
A program may use at most 64 MiB of HBM per device.

v0:
```python
import functools

import jax
import jax.numpy as jnp
from jax import lax
from jax.experimental import pallas as pl
from jax.experimental.pallas import tpu as pltpu
from jax.sharding import PartitionSpec as P

STEPS = 2
TRACERS = 2
GRANT = 12 * 2**20


def call(kernel, name, out_shapes, operands, scratch=()):
    vmem = pl.BlockSpec(memory_space=pltpu.VMEM)
    return pl.pallas_call(
        kernel,
        name=name,
        out_shape=[jax.ShapeDtypeStruct(shape, jnp.float32) for shape in out_shapes],
        in_specs=[vmem] * len(operands),
        out_specs=[vmem] * len(out_shapes),
        scratch_shapes=[pltpu.VMEM(shape, jnp.float32) for shape in scratch],
        compiler_params=pltpu.CompilerParams(vmem_limit_bytes=GRANT),
    )(*operands)


def span(ref, index, rows):
    return ref[pl.ds(index * rows, rows), :]


def pack_kernel(levels, places, thickness_ref, diffusivity_ref, counts_ref, *out_refs):
    me = lax.axis_index("lev")
    counts = counts_ref[...]
    last = thickness_ref.shape[0] - 1
    for distance in range(places):
        start = (me ^ distance) * levels
        out = out_refs[distance]
        for k in range(levels):
            out[k] = thickness_ref[start + k]
        for k in range(levels + 1):
            level = jnp.full(counts.shape, start + k, jnp.int32)
            wet = (level >= 1) & (level < counts)
            out[levels + k] = jnp.where(wet, diffusivity_ref[jnp.minimum(start + k, last)], 0.0)


def local_solve(levels, rows, read, u_ref, b_ref, rp_ref, a_ref, c_ref):
    for tracer in range(TRACERS):
        carried = None
        for k in range(levels):
            here = read(tracer, k) * span(rp_ref, k, rows)
            if k:
                here = here + span(a_ref, k, rows) * carried
            u_ref[pl.ds((tracer * levels + k) * rows, rows), :] = here
            carried = here
        b_ref[pl.ds((TRACERS + tracer) * rows, rows), :] = carried
        for k in range(levels - 2, -1, -1):
            carried = span(u_ref, tracer * levels + k, rows) + span(c_ref, k, rows) * carried
            u_ref[pl.ds((tracer * levels + k) * rows, rows), :] = carried
        b_ref[pl.ds(tracer * rows, rows), :] = carried


def first_kernel(levels, places, strip, *refs):
    parts, refs = refs[:places], refs[places:]
    adj_ref, u_ref, b_ref, rp_ref, a_ref, c_ref, t_ref, tv_ref, tw_ref, i_ref = refs
    rows = strip * places
    me = lax.axis_index("lev")
    for place in range(places):

        @pl.when(me == place)
        def _():
            for distance in range(places):
                offset = (place ^ distance) * strip
                part = parts[distance]
                for k in range(levels):
                    t_ref[pl.ds(k * rows + offset, strip), :] = part[k]
                for k in range(levels + 1):
                    i_ref[pl.ds(k * rows + offset, strip), :] = part[levels + k]

    inner = span(i_ref, 0, rows)
    high = span(t_ref, 0, rows) + inner
    low = jnp.ones_like(high)
    v = None
    for k in range(levels):
        outer = span(i_ref, k + 1, rows)
        ahead = high + outer * low
        rp = low / ahead
        a = inner * rp
        at = pl.ds(k * rows, rows)
        rp_ref[at, :] = rp
        a_ref[at, :] = a
        c_ref[at, :] = outer * rp
        v = a * v if k else a
        tv_ref[at, :] = v
        if k < levels - 1:
            high = span(t_ref, k + 1, rows) * ahead + outer * high
            low = ahead
            inner = outer
    w = span(c_ref, levels - 1, rows)
    base = 2 * TRACERS
    b_ref[pl.ds((base + 1) * rows, rows), :] = v
    b_ref[pl.ds((base + 3) * rows, rows), :] = w
    for k in range(levels - 1, -1, -1):
        at = pl.ds(k * rows, rows)
        if k < levels - 1:
            c = span(c_ref, k, rows)
            v = span(tv_ref, k, rows) + c * v
            w = c * w
        t = span(t_ref, k, rows)
        tv_ref[at, :] = t * v
        tw_ref[at, :] = t * w
    b_ref[pl.ds(base * rows, rows), :] = v
    b_ref[pl.ds((base + 2) * rows, rows), :] = w
    local_solve(
        levels, rows, lambda tracer, k: span(adj_ref, tracer * levels + k, rows), u_ref, b_ref, rp_ref, a_ref, c_ref
    )


def pair_values(rows, odd, mine_ref, other_ref, spikes_ref, other_spikes_ref):
    base = 2 * TRACERS
    mine = [span(mine_ref, i, rows) for i in range(base)] + [span(spikes_ref, base + i, rows) for i in range(4)]
    other = [span(other_ref, i, rows) for i in range(base)] + [span(other_spikes_ref, base + i, rows) for i in range(4)]
    upper = [jnp.where(odd, o, m) for m, o in zip(mine, other)]
    lower = [jnp.where(odd, m, o) for m, o in zip(mine, other)]
    return upper, lower


def merge_kernel(rows, with_spikes, mine_ref, other_ref, spikes_ref, other_spikes_ref, out_ref):
    me = lax.axis_index("lev")
    p, q = pair_values(rows, (me & 1) == 1, mine_ref, other_ref, spikes_ref, other_spikes_ref)
    is_upper = me < 2
    base = 2 * TRACERS
    vf_p, vl_p, wf_p, wl_p = p[base:]
    vf_q, vl_q, wf_q, wl_q = q[base:]
    det = 1.0 / (1.0 - vf_q * wl_p)
    for tracer in range(TRACERS):
        uf_p, ul_p = p[tracer], p[TRACERS + tracer]
        uf_q, ul_q = q[tracer], q[TRACERS + tracer]
        down = ul_q + vl_q * ((ul_p + wl_p * uf_q) * det)
        up = uf_p + wf_p * ((uf_q + vf_q * ul_p) * det)
        out_ref[pl.ds(tracer * rows, rows), :] = jnp.where(is_upper, down, up)
    if with_spikes:
        down = wl_q + vl_q * (wl_p * wf_q * det)
        up = vf_p + wf_p * (vf_q * vl_p * det)
        out_ref[pl.ds(TRACERS * rows, rows), :] = jnp.where(is_upper, down, up)


def finish_kernel(levels, rows, lat_two_ways, fold_apart, *refs):
    (
        mine_ref, other_ref, spikes_ref, other_spikes_ref, near_ref, far_ref, near_beta_ref, far_beta_ref,
        u_ref, t_ref, tv_ref, tw_ref, mask_ref, stencil_ref, source_ref,
    ) = refs[:15]
    out_refs, (masked_ref, fold_ref) = refs[15:-2], refs[-2:]
    vertical_ref, lon_ref, lat_ref = out_refs[:3]
    me = lax.axis_index("lev")
    odd = (me & 1) == 1
    is_upper = me < 2
    p, q = pair_values(rows, odd, mine_ref, other_ref, spikes_ref, other_spikes_ref)
    base = 2 * TRACERS
    vf_p, vl_p, wf_p, wl_p = p[base:]
    vf_q, vl_q, wf_q, wl_q = q[base:]
    det = 1.0 / (1.0 - vf_q * wl_p)
    beta, far_beta = span(near_beta_ref, TRACERS, rows), span(far_beta_ref, TRACERS, rows)
    far_det = 1.0 / (1.0 - beta * far_beta)
    zero = jnp.zeros_like(det)
    lane = lax.broadcasted_iota(jnp.int32, (rows, 128), 1)
    packed = zero
    for tracer in range(TRACERS):
        outside = (span(far_ref, tracer, rows) + far_beta * span(near_ref, tracer, rows)) * far_det
        above = jnp.where(is_upper, zero, outside)
        below = jnp.where(is_upper, outside, zero)
        last_p = p[TRACERS + tracer] + vl_p * above
        first_q = q[tracer] + wf_q * below
        previous = jnp.where(odd, (last_p + wl_p * first_q) * det, above)
        following = jnp.where(odd, below, (first_q + vf_q * last_p) * det)
        for k in range(levels):
            j = tracer * levels + k
            at = pl.ds(j * rows, rows)
            vertical = (
                span(t_ref, k, rows) * span(u_ref, j, rows)
                + span(tv_ref, k, rows) * previous
                + span(tw_ref, k, rows) * following
            )
            vertical_ref[at, :] = vertical
            masked = span(mask_ref, k, rows).astype(jnp.float32) * vertical
            masked_ref[at, :] = masked
            packed = jnp.where((lane >> 1) == j, pltpu.roll(masked, 2 * j + 1, 1), packed)
    lon_ref[pl.ds(0, rows), :] = packed
    lat_odd = (lax.axis_index("lat") & 1) == 1
    fold_ref[...] = jnp.zeros_like(fold_ref)
    weight = stencil_ref[pl.ds(3 * levels * rows + rows - 1, levels, stride=rows), :]
    for tracer in range(TRACERS):
        first = masked_ref[pl.ds(tracer * levels * rows, levels, stride=rows), :]
        last = masked_ref[pl.ds(tracer * levels * rows + rows - 1, levels, stride=rows), :]
        at = pl.ds(tracer * 24, levels)
        lat_ref[at, :] = jnp.where(lat_odd, first, last)
        if lat_two_ways:
            out_refs[3][at, :] = jnp.where(lat_odd, last, first)
        fold_ref[at, :] = weight * last
    source = source_ref[...]
    for i in range(TRACERS * 3):
        moved = jnp.take_along_axis(fold_ref[pl.ds(i * 8, 8), :], source, axis=1)
        if fold_apart:
            out_refs[-1][pl.ds(i * 8, 8), :] = moved
        else:
            lon_ref[pl.ds(rows + i * 8, 8), :] = moved


def tendency_parts(levels, rows, lat_two_ways, fold_apart, refs, masked_ref):
    vertical_ref, mask_ref, stencil_ref, wide_ref, near_ref, lat_ref = refs[:6]
    stride = rows + 8
    lon_odd = (lax.axis_index("lon") & 1) == 1
    lat_odd = (lax.axis_index("lat") & 1) == 1
    is_top = lax.axis_index("lat") == lax.axis_size("lat") - 1
    lane = lax.broadcasted_iota(jnp.int32, (rows, 128), 1)
    row = lax.broadcasted_iota(jnp.int32, (rows, 128), 0)
    wide, near = wide_ref[pl.ds(0, rows), :], near_ref[...]
    east, west = jnp.where(lon_odd, wide, near), jnp.where(lon_odd, near, wide)
    edges = jnp.where((lane & 1) == 0, pltpu.roll(east, 127, 1), pltpu.roll(west, 1, 1))
    fold_ref, fold_at = (refs[-1], 0) if fold_apart else (wide_ref, rows)
    for tracer in range(TRACERS):
        rows_at = pl.ds(tracer * 24, levels)
        halo = lat_ref[rows_at, :]
        back = refs[6][rows_at, :] if lat_two_ways else jnp.zeros_like(halo)
        north, south = jnp.where(lat_odd, back, halo), jnp.where(lat_odd, halo, back)
        masked_ref[pl.ds(tracer * levels * stride + 7, levels, stride=stride), :] = south
        masked_ref[pl.ds((tracer * levels + 1) * stride, levels, stride=stride), :] = north
        for k in range(levels):
            j = tracer * levels + k
            masked_ref[pl.ds(j * stride + 8, rows), :] = span(mask_ref, k, rows).astype(jnp.float32) * span(
                vertical_ref, j, rows
            )

    def next_adjoint(tracer, k):
        j = tracer * levels + k
        mask = span(mask_ref, k, rows).astype(jnp.float32)
        masked = masked_ref[pl.ds(j * stride + 8, rows), :]
        from_north = masked_ref[pl.ds(j * stride + 9, rows), :]
        from_south = masked_ref[pl.ds(j * stride + 7, rows), :]
        edge = pltpu.roll(edges, 127 - 2 * j, 1)
        from_east = jnp.where(lane == 127, edge, pltpu.roll(masked, 127, 1))
        from_west = jnp.where(lane == 0, edge, pltpu.roll(masked, 1, 1))
        weight = [span(stencil_ref, i * levels + k, rows) for i in range(5)]
        tendency = (
            weight[0] * masked
            + weight[1] * from_east
            + weight[2] * from_west
            + weight[3] * from_north
            + weight[4] * from_south
        )
        folded = fold_ref[pl.ds(fold_at + tracer * 24 + k, 1), :]
        tendency = tendency + jnp.where((row == rows - 1) & is_top, folded, 0.0)
        return span(vertical_ref, j, rows) + mask * tendency

    return next_adjoint


def turn_kernel(levels, rows, lat_two_ways, fold_apart, *refs):
    *refs, rp_ref, a_ref, c_ref, u_ref, b_ref, masked_ref = refs
    read = tendency_parts(levels, rows, lat_two_ways, fold_apart, refs, masked_ref)
    local_solve(levels, rows, read, u_ref, b_ref, rp_ref, a_ref, c_ref)


def last_kernel(levels, rows, lat_two_ways, fold_apart, *refs):
    *refs, out_ref, masked_ref = refs
    read = tendency_parts(levels, rows, lat_two_ways, fold_apart, refs, masked_ref)
    for tracer in range(TRACERS):
        for k in range(levels):
            out_ref[pl.ds((tracer * levels + k) * rows, rows), :] = read(tracer, k)


def shards(adj_final, stencil, landmask, thickness, diffusivity, level_counts, fold_partner):
    lat_count, lon_count, places = (lax.axis_size(axis) for axis in ("lat", "lon", "lev"))
    _, levels, rows, width = adj_final.shape
    strip = thickness.shape[1]
    assert places == 4 and width == 128 and strip * places == rows and lon_count % 2 == 0 and lat_count % 2 == 0
    assert 2 * TRACERS * levels <= width and levels <= 24
    flat = (TRACERS * levels * rows, width)
    column = (levels * rows, width)
    adj = adj_final.reshape(flat)
    weights = stencil.reshape(5 * levels * rows, width)
    mask = landmask.reshape(column)

    def lev_swap(value, distance):
        return lax.ppermute(value, "lev", [(i, i ^ distance) for i in range(places)])

    near_pairs = [(i, i ^ 1) for i in range(lon_count)]
    wide_pairs = [(i, (i + 1 if i % 2 else i - 1) % lon_count) for i in range(lon_count)]
    fold_pairs = [(i, lon_count - 1 - i) for i in range(lon_count)]
    fold_apart = wide_pairs != fold_pairs
    lat_two_ways = lat_count > 2
    lat_near = [(i, i ^ 1) for i in range(lat_count)]
    lat_wide = [pair for i in range(1, lat_count - 1, 2) for pair in ((i, i + 1), (i + 1, i))]

    parts = call(
        functools.partial(pack_kernel, levels, places),
        "pack_columns",
        [(2 * levels + 1, strip, width)] * places,
        (thickness, diffusivity, level_counts),
    )
    parts = [parts[0]] + [lev_swap(parts[distance], distance) for distance in range(1, places)]

    targets = fold_partner - (lon_count - 1 - lax.axis_index("lon")) * width
    here = lax.broadcasted_iota(jnp.int32, (width, width), 0)
    hit = targets[:, None] == lax.broadcasted_iota(jnp.int32, (width, width), 1)
    source = jnp.broadcast_to(jnp.sum(jnp.where(hit, here, 0), axis=0)[None], (8, width))

    solved, ends, rp, a, c, t, tv, tw = call(
        functools.partial(first_kernel, levels, places, strip),
        "first_solve",
        [flat, (8 * rows, width)] + [column] * 6,
        (*parts, adj),
        [((levels + 1) * rows, width)],
    )
    spikes = other_spikes = beta = far_beta = None
    for turn_index in range(STEPS):
        first = turn_index == 0
        other = lev_swap(ends, 1)
        if first:
            spikes, other_spikes = ends, other
        near = call(
            functools.partial(merge_kernel, rows, first),
            "merge_pair",
            [((TRACERS + first) * rows, width)],
            (ends, other, spikes, other_spikes),
        )[0]
        far = lev_swap(near, 2)
        if first:
            beta, far_beta = near, far
        messages = [((rows + (0 if fold_apart else 48)), width), (48, width)]
        messages += [(48, width)] * (lat_two_ways + fold_apart)
        vertical, lon_message, lat_message, *rest = call(
            functools.partial(finish_kernel, levels, rows, lat_two_ways, fold_apart),
            "finish_solve",
            [flat] + messages,
            (ends, other, spikes, other_spikes, near, far, beta, far_beta, solved, t, tv, tw, mask, weights, source),
            [flat, (48, width)],
        )
        from_lat = lax.ppermute(lat_message, "lat", lat_near)
        from_wide = lax.ppermute(lon_message, "lon", wide_pairs)
        from_near = lax.ppermute(lon_message[:rows], "lon", near_pairs)
        extra = []
        if lat_two_ways:
            extra.append(lax.ppermute(rest[0], "lat", lat_wide))
        if fold_apart:
            extra.append(lax.ppermute(rest[-1], "lon", fold_pairs))
        operands = (vertical, mask, weights, from_wide, from_near, from_lat, *extra)
        pad = (TRACERS * levels * (rows + 8) + 8, width)
        if turn_index < STEPS - 1:
            solved, ends = call(
                functools.partial(turn_kernel, levels, rows, lat_two_ways, fold_apart),
                "transport_and_solve",
                [flat, (4 * rows, width)],
                (*operands, rp, a, c),
                [pad],
            )
        else:
            out = call(
                functools.partial(last_kernel, levels, rows, lat_two_ways, fold_apart),
                "transport",
                [flat],
                operands,
                [pad],
            )[0]
    return out.reshape(adj_final.shape)


def solution(mesh):
    in_specs = (
        P(None, "lev", "lat", "lon"),
        P(None, "lev", "lat", "lon"),
        P("lev", "lat", "lon"),
        P(None, ("lat", "lev"), "lon"),
        P(None, ("lat", "lev"), "lon"),
        P(("lat", "lev"), "lon"),
        P("lon"),
    )
    out_specs = P(None, "lev", "lat", "lon")
    return jax.shard_map(shards, mesh=mesh, in_specs=in_specs, out_specs=out_specs, check_vma=False)
```

profile of v0, /device:TPU:0, one launch (start us, length us, event | category | flops | bytes accessed | tf_op | source)
XLA Modules:
  0.0 42.7 jit_solution(2945168795955885138)
XLA Ops:
  0.0 0.0 copy-start.2
  0.0 0.0 copy-start.3
  0.0 1.0 %copy-done.3 = f32[72,4,128]{2,1,0:T(4,128)S(1)} copy-done((f32[72,4,128]{2,1,0:T(4,128)S(1)}, f32[72,4,128]{2,1,0:T(4,128)}, u32[]{:S(2)}) %copy-start.3) | copy-done | bytes 147480
  1.0 0.0 copy-start.4
  1.0 0.9 %copy-done.4 = f32[72,4,128]{2,1,0:T(4,128)S(1)} copy-done((f32[72,4,128]{2,1,0:T(4,128)S(1)}, f32[72,4,128]{2,1,0:T(4,128)}, u32[]{:S(2)}) %copy-start.4) | copy-done | bytes 147480
  1.9 0.0 copy-start.5
  1.9 0.7 %copy-done.5 = s32[4,128]{1,0:T(4,128)S(1)} copy-done((s32[4,128]{1,0:T(4,128)S(1)}, s32[4,128]{1,0:T(4,128)}, u32[]{:S(2)}) %copy-start.5) | copy-done | bytes 2072
  2.6 0.0 copy-start
  2.6 0.1 pack_columns.1
  2.7 3.1 %collective-permute-start = (f32[37,4,128]{2,1,0:T(4,128)S(1)}, f32[37,4,128]{2,1,0:T(4,128)S(1)}, u32[]{:S(2)}, u32[]{:S(2)}) collective-permute-start(f32[37,4,128]{2,1,0:T(4,128)S(1)} %get-tuple-element.26), channel_id=1, source_target_pairs={{0,1},{1,0},{2,3},{3,2},{4,5},{5,4},{6,7},{7,6},{8,9},{9,8},{10,11... | collective-permute-start | bytes 227336 | tf_op jit(solution)/shard_map/ppermute | solution.py:285
  5.8 2.6 %collective-permute-start.1 = (f32[37,4,128]{2,1,0:T(4,128)S(1)}, f32[37,4,128]{2,1,0:T(4,128)S(1)}, u32[]{:S(2)}, u32[]{:S(2)}) collective-permute-start(f32[37,4,128]{2,1,0:T(4,128)S(1)} %get-tuple-element.27), channel_id=1, source_target_pairs={{0,2},{1,3},{2,0},{3,1},{4,6},{5,7},{6,4},{7,5},{8,10},{9,11},{10,... | collective-permute-start | bytes 227336 | tf_op jit(solution)/shard_map/ppermute | solution.py:285
  8.4 0.0 collective-permute-start.2
  8.4 0.0 collective-permute-done.refs_1_
  8.4 5.3 %collective-permute-done.1.refs_2_ = f32[37,4,128]{2,1,0:T(4,128)S(1)} collective-permute-done((f32[37,4,128]{2,1,0:T(4,128)S(1)}, f32[37,4,128]{2,1,0:T(4,128)S(1)}, u32[]{:S(2)}, u32[]{:S(2)}) %collective-permute-start.1) | collective-permute-done | bytes 75808 | tf_op jit(solution)/shard_map/ppermute | solution.py:285
  13.7 0.9 %collective-permute-done.2.refs_3_ = f32[37,4,128]{2,1,0:T(4,128)S(1)} collective-permute-done((f32[37,4,128]{2,1,0:T(4,128)S(1)}, f32[37,4,128]{2,1,0:T(4,128)S(1)}, u32[]{:S(2)}, u32[]{:S(2)}) %collective-permute-start.2) | collective-permute-done | bytes 75808 | tf_op jit(solution)/shard_map/ppermute | solution.py:285
  14.6 0.0 copy-done.2
  14.6 0.3 first_solve.1
  14.9 1.3 %collective-permute-start.3 = (f32[128,128]{1,0:T(8,128)S(1)}, f32[128,128]{1,0:T(8,128)S(1)}, u32[]{:S(2)}, u32[]{:S(2)}) collective-permute-start(f32[128,128]{1,0:T(8,128)S(1)} %get-tuple-element.29.mine_ref.spikes_ref.refs_0_.refs_2_), channel_id=1, source_target_pairs={{0,1},{1,0},{2,3},{3,2},{4,5},{5,4},{6,7},{7,6},{8,9},{9,8},{10,11... | collective-permute-start | bytes 196616 | tf_op jit(solution)/shard_map/ppermute | solution.py:285
  16.2 0.7 %broadcast_subtract_fusion = s32[128]{0:T(128)S(1)} fusion(s32[128]{0:T(128)} %param.13, s32[]{:T(128)S(6)} %mul.3), kind=kLoop, calls=%fused_computation.2 | loop fusion | flops 128 | bytes 1028 | tf_op jit(solution)/shard_map/sub | solution.py:303
  16.9 0.0 copy-start.1
  16.9 2.4 %collective-permute-done.3.other_ref.other_spikes_ref.refs_1_.refs_3_ = f32[128,128]{1,0:T(8,128)S(1)} collective-permute-done((f32[128,128]{1,0:T(8,128)S(1)}, f32[128,128]{1,0:T(8,128)S(1)}, u32[]{:S(2)}, u32[]{:S(2)}) %collective-permute-start.3) | collective-permute-done | bytes 65568 | tf_op jit(solution)/shard_map/ppermute | solution.py:285
  19.3 2.6 %collective-permute-start.4 = (f32[48,128]{1,0:T(8,128)S(1)}, f32[48,128]{1,0:T(8,128)S(1)}, u32[]{:S(2)}, u32[]{:S(2)}) collective-permute-start(f32[48,128]{1,0:T(8,128)S(1)} %merge_pair.2.refs_4_.refs_6_), channel_id=1, source_target_pairs={{0,2},{1,3},{2,0},{3,1},{4,6},{5,7},{6,4},{7,5},{8,10},{9,11},{10,... | collective-permute-start | bytes 73736 | tf_op jit(solution)/shard_map/ppermute | solution.py:285
  21.8 0.1 select_reduce_fusion
  21.9 2.1 %collective-permute-done.4.refs_5_.refs_7_ = f32[48,128]{1,0:T(8,128)S(1)} collective-permute-done((f32[48,128]{1,0:T(8,128)S(1)}, f32[48,128]{1,0:T(8,128)S(1)}, u32[]{:S(2)}, u32[]{:S(2)}) %collective-permute-start.4) | collective-permute-done | bytes 24608 | tf_op jit(solution)/shard_map/ppermute | solution.py:285
  24.1 0.0 copy-done
  24.1 0.0 copy-done.1
  24.1 0.2 finish_solve.2
  24.3 0.1 collective-permute-start.5
  24.4 1.6 %collective-permute-start.7 = (f32[48,128]{1,0:T(8,128)S(1)}, f32[48,128]{1,0:T(8,128)S(1)}, u32[]{:S(2)}, u32[]{:S(2)}) collective-permute-start(f32[48,128]{1,0:T(8,128)S(1)} %get-tuple-element.36), channel_id=1, source_target_pairs={{0,16},{16,0},{1,17},{17,1},{2,18},{18,2},{3,19},{19,3},{4,20},{20... | collective-permute-start | bytes 73736 | tf_op jit(solution)/shard_map/ppermute | solution.py:339
  25.9 1.3 %collective-permute-start.6 = (f32[16,128]{1,0:T(8,128)S(1)}, f32[16,128]{1,0:T(8,128)S(1)}, u32[]{:S(2)}, u32[]{:S(2)}) collective-permute-start(f32[16,128]{1,0:T(8,128)S(1)} %slice.6), channel_id=1, source_target_pairs={{0,4},{4,0},{8,12},{12,8},{1,5},{5,1},{9,13},{13,9},{2,6},{6,2},{1... | collective-permute-start | bytes 24584 | tf_op jit(solution)/shard_map/ppermute | solution.py:341
  27.2 0.8 %collective-permute-done.6.refs_4_ = f32[16,128]{1,0:T(8,128)S(1)} collective-permute-done((f32[16,128]{1,0:T(8,128)S(1)}, f32[16,128]{1,0:T(8,128)S(1)}, u32[]{:S(2)}, u32[]{:S(2)}) %collective-permute-start.6) | collective-permute-done | bytes 8224 | tf_op jit(solution)/shard_map/ppermute | solution.py:341
  28.0 0.2 collective-permute-done.7.refs_5_
  28.3 0.0 collective-permute-done.5.refs_3_
  28.3 0.5 %transport_and_solve.1 = (f32[576,128]{1,0:T(8,128)S(1)}, f32[64,128]{1,0:T(8,128)S(1)}) custom-call(f32[576,128]{1,0:T(8,128)S(1)} %get-tuple-element.34.refs_0_, s32[288,128]{1,0:T(8,128)S(1)} %bitcast.9, f32[1440,128]{1,0:T(8,128)S(1)} %bitcast.5, f32[64,128]{1,0:T(8,128)S(1)} %collective-permute-done.5.refs_3_, ...), custom_call_target="tpu_custom_call" | custom-call | tf_op jit(solution)/shard_map/transport_and_solve/pallas_call | solution.py:17
  28.7 1.3 %collective-permute-start.8 = (f32[64,128]{1,0:T(8,128)S(1)}, f32[64,128]{1,0:T(8,128)S(1)}, u32[]{:S(2)}, u32[]{:S(2)}) collective-permute-start(f32[64,128]{1,0:T(8,128)S(1)} %get-tuple-element.40.mine_ref.refs_0_), channel_id=1, source_target_pairs={{0,1},{1,0},{2,3},{3,2},{4,5},{5,4},{6,7},{7,6},{8,9},{9,8},{10,11... | collective-permute-start | bytes 98312 | tf_op jit(solution)/shard_map/ppermute | solution.py:285
  30.0 2.7 %collective-permute-done.8.other_ref.refs_1_ = f32[64,128]{1,0:T(8,128)S(1)} collective-permute-done((f32[64,128]{1,0:T(8,128)S(1)}, f32[64,128]{1,0:T(8,128)S(1)}, u32[]{:S(2)}, u32[]{:S(2)}) %collective-permute-start.8) | collective-permute-done | bytes 32800 | tf_op jit(solution)/shard_map/ppermute | solution.py:285
  32.7 2.6 %collective-permute-start.9 = (f32[32,128]{1,0:T(8,128)S(1)}, f32[32,128]{1,0:T(8,128)S(1)}, u32[]{:S(2)}, u32[]{:S(2)}) collective-permute-start(f32[32,128]{1,0:T(8,128)S(1)} %merge_pair.3.refs_4_), channel_id=1, source_target_pairs={{0,2},{1,3},{2,0},{3,1},{4,6},{5,7},{6,4},{7,5},{8,10},{9,11},{10,... | collective-permute-start | bytes 49160 | tf_op jit(solution)/shard_map/ppermute | solution.py:285
  35.3 2.1 %collective-permute-done.9.refs_5_ = f32[32,128]{1,0:T(8,128)S(1)} collective-permute-done((f32[32,128]{1,0:T(8,128)S(1)}, f32[32,128]{1,0:T(8,128)S(1)}, u32[]{:S(2)}, u32[]{:S(2)}) %collective-permute-start.9) | collective-permute-done | bytes 16416 | tf_op jit(solution)/shard_map/ppermute | solution.py:285
  37.4 0.2 finish_solve.3
  37.7 0.1 collective-permute-start.10
  37.7 1.6 %collective-permute-start.12 = (f32[48,128]{1,0:T(8,128)S(1)}, f32[48,128]{1,0:T(8,128)S(1)}, u32[]{:S(2)}, u32[]{:S(2)}) collective-permute-start(f32[48,128]{1,0:T(8,128)S(1)} %get-tuple-element.44), channel_id=1, source_target_pairs={{0,16},{16,0},{1,17},{17,1},{2,18},{18,2},{3,19},{19,3},{4,20},{20... | collective-permute-start | bytes 73736 | tf_op jit(solution)/shard_map/ppermute | solution.py:339
  39.3 1.3 %collective-permute-start.11 = (f32[16,128]{1,0:T(8,128)S(1)}, f32[16,128]{1,0:T(8,128)S(1)}, u32[]{:S(2)}, u32[]{:S(2)}) collective-permute-start(f32[16,128]{1,0:T(8,128)S(1)} %slice.7), channel_id=1, source_target_pairs={{0,4},{4,0},{8,12},{12,8},{1,5},{5,1},{9,13},{13,9},{2,6},{6,2},{1... | collective-permute-start | bytes 24584 | tf_op jit(solution)/shard_map/ppermute | solution.py:341
  40.6 0.8 %collective-permute-done.11.refs_4_ = f32[16,128]{1,0:T(8,128)S(1)} collective-permute-done((f32[16,128]{1,0:T(8,128)S(1)}, f32[16,128]{1,0:T(8,128)S(1)}, u32[]{:S(2)}, u32[]{:S(2)}) %collective-permute-start.11) | collective-permute-done | bytes 8224 | tf_op jit(solution)/shard_map/ppermute | solution.py:341
  41.4 0.2 collective-permute-done.12.refs_5_
  41.6 0.0 collective-permute-done.10.refs_3_
  41.6 1.1 %transport.1 = f32[576,128]{1,0:T(8,128)} custom-call(f32[576,128]{1,0:T(8,128)S(1)} %get-tuple-element.42.refs_0_, s32[288,128]{1,0:T(8,128)S(1)} %bitcast.11, f32[1440,128]{1,0:T(8,128)S(1)} %bitcast.7, f32[64,128]{1,0:T(8,128)S(1)} %collective-permute-done.10.refs_3_, f32[16,128]{1,0:T(8,128)S(1)} %collective-permute-done.11.refs_4_, ...), custom_call_target="tpu_custom_call" | custom-call | tf_op jit(solution)/shard_map/transport/pallas_call | solution.py:17
  (5 shorter events, 0.1 us)
Async XLA Ops:
  0.0 14.6 %copy-start.2 = (f32[2,18,16,128]{3,2,1,0:T(8,128)S(1)}, f32[2,18,16,128]{3,2,1,0:T(8,128)}, u32[]{:S(2)}) copy-start(f32[2,18,16,128]{3,2,1,0:T(8,128)} %param.7) | copy-start | bytes 884740
  0.0 1.0 %copy-start.3 = (f32[72,4,128]{2,1,0:T(4,128)S(1)}, f32[72,4,128]{2,1,0:T(4,128)}, u32[]{:S(2)}) copy-start(f32[72,4,128]{2,1,0:T(4,128)} %thickness_ref.1) | copy-start | bytes 442372
  1.0 0.9 %copy-start.4 = (f32[72,4,128]{2,1,0:T(4,128)S(1)}, f32[72,4,128]{2,1,0:T(4,128)}, u32[]{:S(2)}) copy-start(f32[72,4,128]{2,1,0:T(4,128)} %diffusivity_ref.1) | copy-start | bytes 442372
  1.9 0.7 %copy-start.5 = (s32[4,128]{1,0:T(4,128)S(1)}, s32[4,128]{1,0:T(4,128)}, u32[]{:S(2)}) copy-start(s32[4,128]{1,0:T(4,128)} %counts_ref.1) | copy-start | bytes 6148
  2.6 21.5 %copy-start = (f32[5,18,16,128]{3,2,1,0:T(8,128)S(1)}, f32[5,18,16,128]{3,2,1,0:T(8,128)}, u32[]{:S(2)}) copy-start(f32[5,18,16,128]{3,2,1,0:T(8,128)} %param.8) | copy-start | bytes 2211844
  2.7 5.7 %collective-permute-start = (f32[37,4,128]{2,1,0:T(4,128)S(1)}, f32[37,4,128]{2,1,0:T(4,128)S(1)}, u32[]{:S(2)}, u32[]{:S(2)}) collective-permute-start(f32[37,4,128]{2,1,0:T(4,128)S(1)} %get-tuple-element.26), channel_id=1, source_target_pairs={{0,1},{1,0},{2,3},{3,2},{4,5},{5,4},{6,7},{7,6},{8,9},{9,8},{10,11... | collective-permute-start | bytes 227336 | tf_op jit(solution)/shard_map/ppermute | solution.py:285
  5.8 7.9 %collective-permute-start.1 = (f32[37,4,128]{2,1,0:T(4,128)S(1)}, f32[37,4,128]{2,1,0:T(4,128)S(1)}, u32[]{:S(2)}, u32[]{:S(2)}) collective-permute-start(f32[37,4,128]{2,1,0:T(4,128)S(1)} %get-tuple-element.27), channel_id=1, source_target_pairs={{0,2},{1,3},{2,0},{3,1},{4,6},{5,7},{6,4},{7,5},{8,10},{9,11},{10,... | collective-permute-start | bytes 227336 | tf_op jit(solution)/shard_map/ppermute | solution.py:285
  8.4 6.3 %collective-permute-start.2 = (f32[37,4,128]{2,1,0:T(4,128)S(1)}, f32[37,4,128]{2,1,0:T(4,128)S(1)}, u32[]{:S(2)}, u32[]{:S(2)}) collective-permute-start(f32[37,4,128]{2,1,0:T(4,128)S(1)} %get-tuple-element.28), channel_id=1, source_target_pairs={{0,3},{1,2},{2,1},{3,0},{4,7},{5,6},{6,5},{7,4},{8,11},{9,10},{10,... | collective-permute-start | bytes 227336 | tf_op jit(solution)/shard_map/ppermute | solution.py:285
  14.9 4.3 %collective-permute-start.3 = (f32[128,128]{1,0:T(8,128)S(1)}, f32[128,128]{1,0:T(8,128)S(1)}, u32[]{:S(2)}, u32[]{:S(2)}) collective-permute-start(f32[128,128]{1,0:T(8,128)S(1)} %get-tuple-element.29.mine_ref.spikes_ref.refs_0_.refs_2_), channel_id=1, source_target_pairs={{0,1},{1,0},{2,3},{3,2},{4,5},{5,4},{6,7},{7,6},{8,9},{9,8},{10,11... | collective-permute-start | bytes 196616 | tf_op jit(solution)/shard_map/ppermute | solution.py:285
  16.9 7.2 %copy-start.1 = (s32[18,16,128]{2,1,0:T(8,128)S(1)}, s32[18,16,128]{2,1,0:T(8,128)}, u32[]{:S(2)}) copy-start(s32[18,16,128]{2,1,0:T(8,128)} %param.9) | copy-start | bytes 442372
  19.3 4.8 %collective-permute-start.4 = (f32[48,128]{1,0:T(8,128)S(1)}, f32[48,128]{1,0:T(8,128)S(1)}, u32[]{:S(2)}, u32[]{:S(2)}) collective-permute-start(f32[48,128]{1,0:T(8,128)S(1)} %merge_pair.2.refs_4_.refs_6_), channel_id=1, source_target_pairs={{0,2},{1,3},{2,0},{3,1},{4,6},{5,7},{6,4},{7,5},{8,10},{9,11},{10,... | collective-permute-start | bytes 73736 | tf_op jit(solution)/shard_map/ppermute | solution.py:285
  24.3 4.0 %collective-permute-start.5 = (f32[64,128]{1,0:T(8,128)S(1)}, f32[64,128]{1,0:T(8,128)S(1)}, u32[]{:S(2)}, u32[]{:S(2)}) collective-permute-start(f32[64,128]{1,0:T(8,128)S(1)} %get-tuple-element.35), channel_id=1, source_target_pairs={{0,12},{4,8},{8,4},{12,0},{1,13},{5,9},{9,5},{13,1},{2,14},{6,10},... | collective-permute-start | bytes 98312 | tf_op jit(solution)/shard_map/ppermute | solution.py:340
  24.4 3.9 %collective-permute-start.7 = (f32[48,128]{1,0:T(8,128)S(1)}, f32[48,128]{1,0:T(8,128)S(1)}, u32[]{:S(2)}, u32[]{:S(2)}) collective-permute-start(f32[48,128]{1,0:T(8,128)S(1)} %get-tuple-element.36), channel_id=1, source_target_pairs={{0,16},{16,0},{1,17},{17,1},{2,18},{18,2},{3,19},{19,3},{4,20},{20... | collective-permute-start | bytes 73736 | tf_op jit(solution)/shard_map/ppermute | solution.py:339
  25.9 2.1 %collective-permute-start.6 = (f32[16,128]{1,0:T(8,128)S(1)}, f32[16,128]{1,0:T(8,128)S(1)}, u32[]{:S(2)}, u32[]{:S(2)}) collective-permute-start(f32[16,128]{1,0:T(8,128)S(1)} %slice.6), channel_id=1, source_target_pairs={{0,4},{4,0},{8,12},{12,8},{1,5},{5,1},{9,13},{13,9},{2,6},{6,2},{1... | collective-permute-start | bytes 24584 | tf_op jit(solution)/shard_map/ppermute | solution.py:341
  28.7 4.0 %collective-permute-start.8 = (f32[64,128]{1,0:T(8,128)S(1)}, f32[64,128]{1,0:T(8,128)S(1)}, u32[]{:S(2)}, u32[]{:S(2)}) collective-permute-start(f32[64,128]{1,0:T(8,128)S(1)} %get-tuple-element.40.mine_ref.refs_0_), channel_id=1, source_target_pairs={{0,1},{1,0},{2,3},{3,2},{4,5},{5,4},{6,7},{7,6},{8,9},{9,8},{10,11... | collective-permute-start | bytes 98312 | tf_op jit(solution)/shard_map/ppermute | solution.py:285
  32.7 4.7 %collective-permute-start.9 = (f32[32,128]{1,0:T(8,128)S(1)}, f32[32,128]{1,0:T(8,128)S(1)}, u32[]{:S(2)}, u32[]{:S(2)}) collective-permute-start(f32[32,128]{1,0:T(8,128)S(1)} %merge_pair.3.refs_4_), channel_id=1, source_target_pairs={{0,2},{1,3},{2,0},{3,1},{4,6},{5,7},{6,4},{7,5},{8,10},{9,11},{10,... | collective-permute-start | bytes 49160 | tf_op jit(solution)/shard_map/ppermute | solution.py:285
  37.7 4.0 %collective-permute-start.10 = (f32[64,128]{1,0:T(8,128)S(1)}, f32[64,128]{1,0:T(8,128)S(1)}, u32[]{:S(2)}, u32[]{:S(2)}) collective-permute-start(f32[64,128]{1,0:T(8,128)S(1)} %get-tuple-element.43), channel_id=1, source_target_pairs={{0,12},{4,8},{8,4},{12,0},{1,13},{5,9},{9,5},{13,1},{2,14},{6,10},... | collective-permute-start | bytes 98312 | tf_op jit(solution)/shard_map/ppermute | solution.py:340
  37.7 3.9 %collective-permute-start.12 = (f32[48,128]{1,0:T(8,128)S(1)}, f32[48,128]{1,0:T(8,128)S(1)}, u32[]{:S(2)}, u32[]{:S(2)}) collective-permute-start(f32[48,128]{1,0:T(8,128)S(1)} %get-tuple-element.44), channel_id=1, source_target_pairs={{0,16},{16,0},{1,17},{17,1},{2,18},{18,2},{3,19},{19,3},{4,20},{20... | collective-permute-start | bytes 73736 | tf_op jit(solution)/shard_map/ppermute | solution.py:339
  39.3 2.1 %collective-permute-start.11 = (f32[16,128]{1,0:T(8,128)S(1)}, f32[16,128]{1,0:T(8,128)S(1)}, u32[]{:S(2)}, u32[]{:S(2)}) collective-permute-start(f32[16,128]{1,0:T(8,128)S(1)} %slice.7), channel_id=1, source_target_pairs={{0,4},{4,0},{8,12},{12,8},{1,5},{5,1},{9,13},{13,9},{2,6},{6,2},{1... | collective-permute-start | bytes 24584 | tf_op jit(solution)/shard_map/ppermute | solution.py:341
where the time goes:
time: 42.9 us; the launch traced here: 42.7 us
  starting transfers between devices  19.3 us (45%)
  waiting for transfers between devices  17.7 us (41%)
  local copies, waits for them, and re-layouts  2.56 us (6%)
  Pallas kernels  2.41 us (6%)
  other arithmetic  0.75 us (2%)
    ppermute x7, waiting for transfers between devices, lev_swap(): lax.ppermute(value, 'lev', [(i, i ^ distance) for i in range(places)])  15.6 us
    ppermute x7, starting transfers between devices, lev_swap(): lax.ppermute(value, 'lev', [(i, i ^ distance) for i in range(places)])  13.5 us
    ppermute x2, starting transfers between devices, shards(): from_lat = lax.ppermute(lat_message, 'lat', lat_near)  3.11 us
    unnamed x12, local copies, waits for them, and re-layouts  2.56 us
    ppermute x2, starting transfers between devices, shards(): from_near = lax.ppermute(lon_message[:rows], 'lon', near_pairs)  2.55 us
    pallas_call x8, Pallas kernels, call(): pl.pallas_call(kernel, name=name, out_shape=[jax.ShapeDtypeStruct(shape,...  2.41 us
    ppermute x2, waiting for transfers between devices, shards(): from_near = lax.ppermute(lon_message[:rows], 'lon', near_pairs)  1.66 us
  transfers between devices with their start and end apart: 13, of which 10 were waited for; matrix products, arithmetic and copies ran while one was open for 2% of the time, Pallas kernels for 0%

commit v1 on v0

--- a/solution.py
+++ b/solution.py
@@ -12,15 +12,16 @@
 GRANT = 12 * 2**20
 
 
-def call(kernel, name, out_shapes, operands, scratch=()):
-    vmem = pl.BlockSpec(memory_space=pltpu.VMEM)
+def call(kernel, name, out_shapes, operands, scratch=(), copies=0, read_in_place=False, write_in_place=False):
+    vmem, any_space = pl.BlockSpec(memory_space=pltpu.VMEM), pl.BlockSpec(memory_space=pl.ANY)
     return pl.pallas_call(
         kernel,
         name=name,
         out_shape=[jax.ShapeDtypeStruct(shape, jnp.float32) for shape in out_shapes],
-        in_specs=[vmem] * len(operands),
-        out_specs=[vmem] * len(out_shapes),
-        scratch_shapes=[pltpu.VMEM(shape, jnp.float32) for shape in scratch],
+        in_specs=[any_space if read_in_place else vmem] * len(operands),
+        out_specs=[any_space if write_in_place else vmem] * len(out_shapes),
+        scratch_shapes=[pltpu.VMEM(*shape) if isinstance(shape[0], tuple) else pltpu.VMEM(shape, jnp.float32) for shape in scratch]
+        + [pltpu.SemaphoreType.DMA((copies,))] * (copies > 0),
         compiler_params=pltpu.CompilerParams(vmem_limit_bytes=GRANT),
     )(*operands)
 
@@ -29,19 +30,30 @@
     return ref[pl.ds(index * rows, rows), :]
 
 
-def pack_kernel(levels, places, thickness_ref, diffusivity_ref, counts_ref, *out_refs):
+def pack_kernel(levels, places, thickness_ref, diffusivity_ref, counts_ref, *refs):
+    out_refs, (held_ref, held_counts_ref, sems) = refs[:places], refs[places:]
     me = lax.axis_index("lev")
-    counts = counts_ref[...]
-    last = thickness_ref.shape[0] - 1
+    ahead = [
+        pltpu.make_async_copy(counts_ref, held_counts_ref, sems.at[0]),
+        pltpu.make_async_copy(diffusivity_ref, held_ref, sems.at[1]),
+    ]
+    for distance in range(places):
+        source = thickness_ref.at[pl.ds((me ^ distance) * levels, levels)]
+        ahead.append(pltpu.make_async_copy(source, out_refs[distance].at[pl.ds(0, levels)], sems.at[2 + distance]))
+    for copy in ahead:
+        copy.start()
+    for copy in ahead[:2]:
+        copy.wait()
+    counts = held_counts_ref[...]
+    last = held_ref.shape[0] - 1
     for distance in range(places):
         start = (me ^ distance) * levels
-        out = out_refs[distance]
-        for k in range(levels):
-            out[k] = thickness_ref[start + k]
         for k in range(levels + 1):
             level = jnp.full(counts.shape, start + k, jnp.int32)
             wet = (level >= 1) & (level < counts)
-            out[levels + k] = jnp.where(wet, diffusivity_ref[jnp.minimum(start + k, last)], 0.0)
+            out_refs[distance][levels + k] = jnp.where(wet, held_ref[jnp.minimum(start + k, last)], 0.0)
+    for copy in ahead[2:]:
+        copy.wait()
 
 
 def local_solve(levels, rows, read, u_ref, b_ref, rp_ref, a_ref, c_ref):
@@ -125,48 +137,65 @@
     return upper, lower
 
 
-def merge_kernel(rows, with_spikes, mine_ref, other_ref, spikes_ref, other_spikes_ref, out_ref):
-    me = lax.axis_index("lev")
-    p, q = pair_values(rows, (me & 1) == 1, mine_ref, other_ref, spikes_ref, other_spikes_ref)
-    is_upper = me < 2
+def pair_spikes(p, q, is_upper):
     base = 2 * TRACERS
     vf_p, vl_p, wf_p, wl_p = p[base:]
     vf_q, vl_q, wf_q, wl_q = q[base:]
     det = 1.0 / (1.0 - vf_q * wl_p)
-    for tracer in range(TRACERS):
-        uf_p, ul_p = p[tracer], p[TRACERS + tracer]
-        uf_q, ul_q = q[tracer], q[TRACERS + tracer]
-        down = ul_q + vl_q * ((ul_p + wl_p * uf_q) * det)
-        up = uf_p + wf_p * ((uf_q + vf_q * ul_p) * det)
-        out_ref[pl.ds(tracer * rows, rows), :] = jnp.where(is_upper, down, up)
-    if with_spikes:
-        down = wl_q + vl_q * (wl_p * wf_q * det)
-        up = vf_p + wf_p * (vf_q * vl_p * det)
-        out_ref[pl.ds(TRACERS * rows, rows), :] = jnp.where(is_upper, down, up)
-
-
-def finish_kernel(levels, rows, lat_two_ways, fold_apart, *refs):
+    one, zero = jnp.ones_like(det), jnp.zeros_like(det)
+    down, up = vl_q * det, wf_p * det
+    share_p = (jnp.where(is_upper, zero, one), jnp.where(is_upper, down, up * vf_q))
+    share_q = (jnp.where(is_upper, down * wl_p, up), jnp.where(is_upper, one, zero))
+    beta = jnp.where(is_upper, wl_q + down * wl_p * wf_q, vf_p + up * vf_q * vl_p)
+    return det, share_p, share_q, beta
+
+
+def pair_alpha(p, q, share_p, share_q, tracer):
+    return (
+        share_p[0] * p[tracer]
+        + share_p[1] * p[TRACERS + tracer]
+        + share_q[0] * q[tracer]
+        + share_q[1] * q[TRACERS + tracer]
+    )
+
+
+def merge_kernel(rows, mine_ref, other_ref, out_ref, share_ref):
+    me = lax.axis_index("lev")
+    odd = (me & 1) == 1
+    p, q = pair_values(rows, odd, mine_ref, other_ref, mine_ref, other_ref)
+    _, share_p, share_q, beta = pair_spikes(p, q, me < 2)
+    for tracer in range(TRACERS):
+        out_ref[pl.ds(tracer * rows, rows), :] = pair_alpha(p, q, share_p, share_q, tracer)
+    out_ref[pl.ds(TRACERS * rows, rows), :] = beta
+    for i in range(2):
+        share_ref[pl.ds(i * rows, rows), :] = jnp.where(odd, share_q[i], share_p[i])
+
+
+def finish_kernel(levels, rows, lat_two_ways, fold_apart, two_shares, *refs):
     (
-        mine_ref, other_ref, spikes_ref, other_spikes_ref, near_ref, far_ref, near_beta_ref, far_beta_ref,
+        mine_ref, other_ref, spikes_ref, other_spikes_ref, far_ref, more_ref, far_beta_ref,
         u_ref, t_ref, tv_ref, tw_ref, mask_ref, stencil_ref, source_ref,
-    ) = refs[:15]
-    out_refs, (masked_ref, fold_ref) = refs[15:-2], refs[-2:]
+    ) = refs[:14]
+    out_refs, (masked_ref, fold_ref) = refs[14:-2], refs[-2:]
     vertical_ref, lon_ref, lat_ref = out_refs[:3]
     me = lax.axis_index("lev")
     odd = (me & 1) == 1
     is_upper = me < 2
     p, q = pair_values(rows, odd, mine_ref, other_ref, spikes_ref, other_spikes_ref)
     base = 2 * TRACERS
-    vf_p, vl_p, wf_p, wl_p = p[base:]
-    vf_q, vl_q, wf_q, wl_q = q[base:]
-    det = 1.0 / (1.0 - vf_q * wl_p)
-    beta, far_beta = span(near_beta_ref, TRACERS, rows), span(far_beta_ref, TRACERS, rows)
+    vl_p, wl_p = p[base + 1], p[base + 3]
+    vf_q, wf_q = q[base], q[base + 2]
+    det, share_p, share_q, beta = pair_spikes(p, q, is_upper)
+    far_beta = span(far_beta_ref, TRACERS, rows)
     far_det = 1.0 / (1.0 - beta * far_beta)
     zero = jnp.zeros_like(det)
     lane = lax.broadcasted_iota(jnp.int32, (rows, 128), 1)
     packed = zero
     for tracer in range(TRACERS):
-        outside = (span(far_ref, tracer, rows) + far_beta * span(near_ref, tracer, rows)) * far_det
+        far = span(far_ref, tracer, rows)
+        if two_shares:
+            far = far + span(more_ref, tracer, rows)
+        outside = (far + far_beta * pair_alpha(p, q, share_p, share_q, tracer)) * far_det
         above = jnp.where(is_upper, zero, outside)
         below = jnp.where(is_upper, outside, zero)
         last_p = p[TRACERS + tracer] + vl_p * above
@@ -256,17 +285,29 @@
 
 
 def turn_kernel(levels, rows, lat_two_ways, fold_apart, *refs):
-    *refs, rp_ref, a_ref, c_ref, u_ref, b_ref, masked_ref = refs
+    *refs, rp_ref, a_ref, c_ref, share_ref, u_ref, b_ref, far_ref, masked_ref = refs
     read = tendency_parts(levels, rows, lat_two_ways, fold_apart, refs, masked_ref)
     local_solve(levels, rows, read, u_ref, b_ref, rp_ref, a_ref, c_ref)
+    for tracer in range(TRACERS):
+        first, last = span(b_ref, tracer, rows), span(b_ref, TRACERS + tracer, rows)
+        far_ref[pl.ds(tracer * rows, rows), :] = span(share_ref, 0, rows) * first + span(share_ref, 1, rows) * last
 
 
 def last_kernel(levels, rows, lat_two_ways, fold_apart, *refs):
-    *refs, out_ref, masked_ref = refs
+    *refs, out_ref, masked_ref, held_ref, sems = refs
     read = tendency_parts(levels, rows, lat_two_ways, fold_apart, refs, masked_ref)
-    for tracer in range(TRACERS):
-        for k in range(levels):
-            out_ref[pl.ds((tracer * levels + k) * rows, rows), :] = read(tracer, k)
+    copies = []
+    half = (levels + 1) // 2
+    for tracer in range(TRACERS):
+        for first, last in ((0, half), (half, levels)):
+            for k in range(first, last):
+                held_ref[pl.ds((tracer * levels + k) * rows, rows), :] = read(tracer, k)
+            at = pl.ds((tracer * levels + first) * rows, (last - first) * rows)
+            copy = pltpu.make_async_copy(held_ref.at[at], out_ref.at[at], sems.at[len(copies)])
+            copy.start()
+            copies.append(copy)
+    for copy in copies:
+        copy.wait()
 
 
 def shards(adj_final, stencil, landmask, thickness, diffusivity, level_counts, fold_partner):
@@ -292,13 +333,17 @@
     lat_near = [(i, i ^ 1) for i in range(lat_count)]
     lat_wide = [pair for i in range(1, lat_count - 1, 2) for pair in ((i, i + 1), (i + 1, i))]
 
-    parts = call(
+    own, *parts = call(
         functools.partial(pack_kernel, levels, places),
         "pack_columns",
         [(2 * levels + 1, strip, width)] * places,
         (thickness, diffusivity, level_counts),
+        [thickness.shape, (level_counts.shape, jnp.int32)],
+        2 + places,
+        read_in_place=True,
     )
-    parts = [parts[0]] + [lev_swap(parts[distance], distance) for distance in range(1, places)]
+    parts = [lev_swap(parts[distance - 1], distance) for distance in range(places - 1, 0, -1)][::-1]
+    parts = [own] + parts
 
     targets = fold_partner - (lon_count - 1 - lax.axis_index("lon")) * width
     here = lax.broadcasted_iota(jnp.int32, (width, width), 0)
@@ -312,28 +357,27 @@
         (*parts, adj),
         [((levels + 1) * rows, width)],
     )
-    spikes = other_spikes = beta = far_beta = None
     for turn_index in range(STEPS):
-        first = turn_index == 0
-        other = lev_swap(ends, 1)
-        if first:
+        if turn_index == 0:
+            other = lev_swap(ends, 1)
+            near, share = call(
+                functools.partial(merge_kernel, rows),
+                "merge_pair",
+                [((TRACERS + 1) * rows, width), (2 * rows, width)],
+                (ends, other),
+            )
+            far = more = far_beta = lev_swap(near, 2)
             spikes, other_spikes = ends, other
-        near = call(
-            functools.partial(merge_kernel, rows, first),
-            "merge_pair",
-            [((TRACERS + first) * rows, width)],
-            (ends, other, spikes, other_spikes),
-        )[0]
-        far = lev_swap(near, 2)
-        if first:
-            beta, far_beta = near, far
+        else:
+            more, far = lev_swap(alpha, 3), lev_swap(alpha, 2)
+            other = lev_swap(ends, 1)
         messages = [((rows + (0 if fold_apart else 48)), width), (48, width)]
         messages += [(48, width)] * (lat_two_ways + fold_apart)
         vertical, lon_message, lat_message, *rest = call(
-            functools.partial(finish_kernel, levels, rows, lat_two_ways, fold_apart),
+            functools.partial(finish_kernel, levels, rows, lat_two_ways, fold_apart, turn_index > 0),
             "finish_solve",
             [flat] + messages,
-            (ends, other, spikes, other_spikes, near, far, beta, far_beta, solved, t, tv, tw, mask, weights, source),
+            (ends, other, spikes, other_spikes, far, more, far_beta, solved, t, tv, tw, mask, weights, source),
             [flat, (48, width)],
         )
         from_lat = lax.ppermute(lat_message, "lat", lat_near)
@@ -347,11 +391,11 @@
         operands = (vertical, mask, weights, from_wide, from_near, from_lat, *extra)
         pad = (TRACERS * levels * (rows + 8) + 8, width)
         if turn_index < STEPS - 1:
-            solved, ends = call(
+            solved, ends, alpha = call(
                 functools.partial(turn_kernel, levels, rows, lat_two_ways, fold_apart),
                 "transport_and_solve",
-                [flat, (4 * rows, width)],
-                (*operands, rp, a, c),
+                [flat, (4 * rows, width), (2 * rows, width)],
+                (*operands, rp, a, c, share),
                 [pad],
             )
         else:
@@ -360,7 +404,9 @@
                 "transport",
                 [flat],
                 operands,
-                [pad],
+                [pad, flat],
+                4,
+                write_in_place=True,
             )[0]
     return out.reshape(adj_final.shape)
 

time: 42.9 us -> 44.3 us (1.033)
  local copies, waits for them, and re-layouts: 2.56 us -> 3.48 us
  other arithmetic: 0.75 us -> 0.1 us
  waiting for transfers between devices: 17.7 us -> 18.2 us
    unnamed x12 -> x14, local copies, waits for them, and re-layouts: 2.56 us -> 3.48 us
    sub x1, other arithmetic: 0.66 us -> 0.01 us  [shards(): targets = fold_partner - (lon_count - 1 - lax.axis_index('lon')) * width]
    ppermute x7 -> x8, waiting for transfers between devices: 15.6 us -> 16 us  [lev_swap(): lax.ppermute(value, 'lev', [(i, i ^ distance) for i in range(places)])]
    pallas_call x8 -> x7, Pallas kernels: 2.41 us -> 2.81 us  [call(): pl.pallas_call(kernel, name=name, out_shape=[jax.ShapeDtypeStruct(shape,...]
    ppermute x7 -> x8, starting transfers between devices: 13.5 us -> 13.6 us  [lev_swap(): lax.ppermute(value, 'lev', [(i, i ^ distance) for i in range(places)])]
  transfers between devices with their start and end apart: 13 -> 14, of which waited for: 10 -> 10; matrix products, arithmetic and copies ran while one was open for 2% -> 0% of each run, Pallas kernels for 0% -> 0%
where the time goes in v1:
time: 44.3 us; the launch traced here: 44.1 us
  starting transfers between devices  19.4 us (44%)
  waiting for transfers between devices  18.2 us (41%)
  local copies, waits for them, and re-layouts  3.48 us (8%)
  Pallas kernels  2.81 us (6%)
    ppermute x8, waiting for transfers between devices, lev_swap(): lax.ppermute(value, 'lev', [(i, i ^ distance) for i in range(places)])  16 us
    ppermute x8, starting transfers between devices, lev_swap(): lax.ppermute(value, 'lev', [(i, i ^ distance) for i in range(places)])  13.6 us
    unnamed x14, local copies, waits for them, and re-layouts  3.48 us
    ppermute x2, starting transfers between devices, shards(): from_lat = lax.ppermute(lat_message, 'lat', lat_near)  3.11 us
    pallas_call x7, Pallas kernels, call(): pl.pallas_call(kernel, name=name, out_shape=[jax.ShapeDtypeStruct(shape,...  2.81 us
    ppermute x2, starting transfers between devices, shards(): from_near = lax.ppermute(lon_message[:rows], 'lon', near_pairs)  2.55 us
    ppermute x2, waiting for transfers between devices, shards(): from_near = lax.ppermute(lon_message[:rows], 'lon', near_pairs)  1.66 us
  transfers between devices with their start and end apart: 14, of which 10 were waited for; matrix products, arithmetic and copies ran while one was open for 0% of the time, Pallas kernels for 0%

profile of v1, /device:TPU:0, one launch (start us, length us, event | category | flops | bytes accessed | tf_op | source)
XLA Modules:
  0.0 44.1 jit_solution(4589991332206567277)
XLA Ops:
  0.0 0.0 copy-start.3
  0.0 0.9 %copy-done.3 = f32[72,4,128]{2,1,0:T(4,128)S(1)} copy-done((f32[72,4,128]{2,1,0:T(4,128)S(1)}, f32[72,4,128]{2,1,0:T(4,128)}, u32[]{:S(2)}) %copy-start.3) | copy-done | bytes 147480
  0.9 0.0 copy-start.4
  0.9 0.9 %copy-done.4 = f32[72,4,128]{2,1,0:T(4,128)S(1)} copy-done((f32[72,4,128]{2,1,0:T(4,128)S(1)}, f32[72,4,128]{2,1,0:T(4,128)}, u32[]{:S(2)}) %copy-start.4) | copy-done | bytes 147480
  1.8 0.0 copy-start.5
  1.8 0.7 %copy-done.5 = s32[4,128]{1,0:T(4,128)S(1)} copy-done((s32[4,128]{1,0:T(4,128)S(1)}, s32[4,128]{1,0:T(4,128)}, u32[]{:S(2)}) %copy-start.5) | copy-done | bytes 2072
  2.5 0.0 copy-start
  2.5 0.5 %pack_columns.1 = (f32[37,4,128]{2,1,0:T(4,128)S(1)}, f32[37,4,128]{2,1,0:T(4,128)S(1)}, f32[37,4,128]{2,1,0:T(4,128)S(1)}, f32[37,4,128]{2,1,0:T(4,128)S(1)}) custom-call(f32[72,4,128]{2,1,0:T(4,128)S(1)} %copy-done.3, f32[72,4,128]{2,1,0:T(4,128)S(1)} %copy-done.4, s32[4,128]{1,0:T(4,128)S(1)} %copy-done.5), custom_call_target="tpu_custom_call" | custom-call | tf_op jit(solution)/shard_map/pack_columns/pallas_call | solution.py:17
  3.0 3.1 %collective-permute-start = (f32[37,4,128]{2,1,0:T(4,128)S(1)}, f32[37,4,128]{2,1,0:T(4,128)S(1)}, u32[]{:S(2)}, u32[]{:S(2)}) collective-permute-start(f32[37,4,128]{2,1,0:T(4,128)S(1)} %get-tuple-element.29), channel_id=1, source_target_pairs={{0,1},{1,0},{2,3},{3,2},{4,5},{5,4},{6,7},{7,6},{8,9},{9,8},{10,11... | collective-permute-start | bytes 227336 | tf_op jit(solution)/shard_map/ppermute | solution.py:326
  6.2 2.6 %collective-permute-start.1 = (f32[37,4,128]{2,1,0:T(4,128)S(1)}, f32[37,4,128]{2,1,0:T(4,128)S(1)}, u32[]{:S(2)}, u32[]{:S(2)}) collective-permute-start(f32[37,4,128]{2,1,0:T(4,128)S(1)} %get-tuple-element.30), channel_id=1, source_target_pairs={{0,2},{1,3},{2,0},{3,1},{4,6},{5,7},{6,4},{7,5},{8,10},{9,11},{10,... | collective-permute-start | bytes 227336 | tf_op jit(solution)/shard_map/ppermute | solution.py:326
  8.7 0.0 collective-permute-start.2
  8.7 0.0 collective-permute-done.refs_1_
  8.7 5.3 %collective-permute-done.1.refs_2_ = f32[37,4,128]{2,1,0:T(4,128)S(1)} collective-permute-done((f32[37,4,128]{2,1,0:T(4,128)S(1)}, f32[37,4,128]{2,1,0:T(4,128)S(1)}, u32[]{:S(2)}, u32[]{:S(2)}) %collective-permute-start.1) | collective-permute-done | bytes 75808 | tf_op jit(solution)/shard_map/ppermute | solution.py:326
  14.1 0.9 %collective-permute-done.2.refs_3_ = f32[37,4,128]{2,1,0:T(4,128)S(1)} collective-permute-done((f32[37,4,128]{2,1,0:T(4,128)S(1)}, f32[37,4,128]{2,1,0:T(4,128)S(1)}, u32[]{:S(2)}, u32[]{:S(2)}) %collective-permute-start.2) | collective-permute-done | bytes 75808 | tf_op jit(solution)/shard_map/ppermute | solution.py:326
  15.0 0.0 copy-start.2
  15.0 1.0 %copy-done.2 = f32[2,18,16,128]{3,2,1,0:T(8,128)S(1)} copy-done((f32[2,18,16,128]{3,2,1,0:T(8,128)S(1)}, f32[2,18,16,128]{3,2,1,0:T(8,128)}, u32[]{:S(2)}) %copy-start.2) | copy-done | bytes 294936
  16.0 0.0 copy-start.6
  16.0 0.3 first_solve.1
  16.2 0.0 copy-start.1
  16.3 1.3 %collective-permute-start.3 = (f32[128,128]{1,0:T(8,128)S(1)}, f32[128,128]{1,0:T(8,128)S(1)}, u32[]{:S(2)}, u32[]{:S(2)}) collective-permute-start(f32[128,128]{1,0:T(8,128)S(1)} %get-tuple-element.32.mine_ref.refs_0_.refs_2_), channel_id=1, source_target_pairs={{0,1},{1,0},{2,3},{3,2},{4,5},{5,4},{6,7},{7,6},{8,9},{9,8},{10,11... | collective-permute-start | bytes 196616 | tf_op jit(solution)/shard_map/ppermute | solution.py:326
  17.6 0.0 copy-done.6
  17.6 3.0 %collective-permute-done.3.other_ref.refs_1_.refs_3_ = f32[128,128]{1,0:T(8,128)S(1)} collective-permute-done((f32[128,128]{1,0:T(8,128)S(1)}, f32[128,128]{1,0:T(8,128)S(1)}, u32[]{:S(2)}, u32[]{:S(2)}) %collective-permute-start.3) | collective-permute-done | bytes 65568 | tf_op jit(solution)/shard_map/ppermute | solution.py:326
  20.6 2.6 %collective-permute-start.4 = (f32[48,128]{1,0:T(8,128)S(1)}, f32[48,128]{1,0:T(8,128)S(1)}, u32[]{:S(2)}, u32[]{:S(2)}) collective-permute-start(f32[48,128]{1,0:T(8,128)S(1)} %get-tuple-element.33), channel_id=1, source_target_pairs={{0,2},{1,3},{2,0},{3,1},{4,6},{5,7},{6,4},{7,5},{8,10},{9,11},{10,... | collective-permute-start | bytes 73736 | tf_op jit(solution)/shard_map/ppermute | solution.py:326
  23.2 0.1 select_reduce_fusion
  23.3 2.1 %collective-permute-done.4.refs_4_.refs_5_.refs_6_ = f32[48,128]{1,0:T(8,128)S(1)} collective-permute-done((f32[48,128]{1,0:T(8,128)S(1)}, f32[48,128]{1,0:T(8,128)S(1)}, u32[]{:S(2)}, u32[]{:S(2)}) %collective-permute-start.4) | collective-permute-done | bytes 24608 | tf_op jit(solution)/shard_map/ppermute | solution.py:326
  25.4 0.0 copy-done
  25.4 0.0 copy-done.1
  25.4 0.2 finish_solve.2
  25.7 0.1 collective-permute-start.5
  25.7 1.6 %collective-permute-start.7 = (f32[48,128]{1,0:T(8,128)S(1)}, f32[48,128]{1,0:T(8,128)S(1)}, u32[]{:S(2)}, u32[]{:S(2)}) collective-permute-start(f32[48,128]{1,0:T(8,128)S(1)} %get-tuple-element.40), channel_id=1, source_target_pairs={{0,16},{16,0},{1,17},{17,1},{2,18},{18,2},{3,19},{19,3},{4,20},{20... | collective-permute-start | bytes 73736 | tf_op jit(solution)/shard_map/ppermute | solution.py:383
  27.3 1.3 %collective-permute-start.6 = (f32[16,128]{1,0:T(8,128)S(1)}, f32[16,128]{1,0:T(8,128)S(1)}, u32[]{:S(2)}, u32[]{:S(2)}) collective-permute-start(f32[16,128]{1,0:T(8,128)S(1)} %slice.6), channel_id=1, source_target_pairs={{0,4},{4,0},{8,12},{12,8},{1,5},{5,1},{9,13},{13,9},{2,6},{6,2},{1... | collective-permute-start | bytes 24584 | tf_op jit(solution)/shard_map/ppermute | solution.py:385
  28.6 0.8 %collective-permute-done.6.refs_4_ = f32[16,128]{1,0:T(8,128)S(1)} collective-permute-done((f32[16,128]{1,0:T(8,128)S(1)}, f32[16,128]{1,0:T(8,128)S(1)}, u32[]{:S(2)}, u32[]{:S(2)}) %collective-permute-start.6) | collective-permute-done | bytes 8224 | tf_op jit(solution)/shard_map/ppermute | solution.py:385
  29.4 0.2 collective-permute-done.7.refs_5_
  29.6 0.0 collective-permute-done.5.refs_3_
  29.6 0.4 %transport_and_solve.1 = (f32[576,128]{1,0:T(8,128)S(1)}, f32[64,128]{1,0:T(8,128)S(1)}, f32[32,128]{1,0:T(8,128)S(1)}) custom-call(f32[576,128]{1,0:T(8,128)S(1)} %get-tuple-element.38.refs_0_, s32[288,128]{1,0:T(8,128)S(1)} %bitcast.9, f32[1440,128]{1,0:T(8,128)S(1)} %bitcast.5, f32[64,128]{1,0:T(8,128)S(1)} %collective-permute-done.5.refs_3_, ...), custom_call_target="tpu_custom_call" | custom-call | tf_op jit(solution)/shard_map/transport_and_solve/pallas_call | solution.py:17
  30.1 1.3 %collective-permute-start.8 = (f32[64,128]{1,0:T(8,128)S(1)}, f32[64,128]{1,0:T(8,128)S(1)}, u32[]{:S(2)}, u32[]{:S(2)}) collective-permute-start(f32[64,128]{1,0:T(8,128)S(1)} %get-tuple-element.45.refs_0_), channel_id=1, source_target_pairs={{0,1},{1,0},{2,3},{3,2},{4,5},{5,4},{6,7},{7,6},{8,9},{9,8},{10,11... | collective-permute-start | bytes 98312 | tf_op jit(solution)/shard_map/ppermute | solution.py:326
  31.4 2.7 %collective-permute-start.10 = (f32[32,128]{1,0:T(8,128)S(1)}, f32[32,128]{1,0:T(8,128)S(1)}, u32[]{:S(2)}, u32[]{:S(2)}) collective-permute-start(f32[32,128]{1,0:T(8,128)S(1)} %get-tuple-element.46), channel_id=1, source_target_pairs={{0,3},{1,2},{2,1},{3,0},{4,7},{5,6},{6,5},{7,4},{8,11},{9,10},{10,... | collective-permute-start | bytes 49160 | tf_op jit(solution)/shard_map/ppermute | solution.py:326
  34.1 0.0 collective-permute-start.9
  34.1 2.8 %collective-permute-done.10.refs_5_ = f32[32,128]{1,0:T(8,128)S(1)} collective-permute-done((f32[32,128]{1,0:T(8,128)S(1)}, f32[32,128]{1,0:T(8,128)S(1)}, u32[]{:S(2)}, u32[]{:S(2)}) %collective-permute-start.10) | collective-permute-done | bytes 16416 | tf_op jit(solution)/shard_map/ppermute | solution.py:326
  36.9 1.8 %collective-permute-done.9.refs_4_ = f32[32,128]{1,0:T(8,128)S(1)} collective-permute-done((f32[32,128]{1,0:T(8,128)S(1)}, f32[32,128]{1,0:T(8,128)S(1)}, u32[]{:S(2)}, u32[]{:S(2)}) %collective-permute-start.9) | collective-permute-done | bytes 16416 | tf_op jit(solution)/shard_map/ppermute | solution.py:326
  38.8 0.0 collective-permute-done.8.refs_1_
  38.8 0.2 finish_solve.3
  39.0 0.1 collective-permute-start.11
  39.1 1.6 %collective-permute-start.13 = (f32[48,128]{1,0:T(8,128)S(1)}, f32[48,128]{1,0:T(8,128)S(1)}, u32[]{:S(2)}, u32[]{:S(2)}) collective-permute-start(f32[48,128]{1,0:T(8,128)S(1)} %get-tuple-element.50), channel_id=1, source_target_pairs={{0,16},{16,0},{1,17},{17,1},{2,18},{18,2},{3,19},{19,3},{4,20},{20... | collective-permute-start | bytes 73736 | tf_op jit(solution)/shard_map/ppermute | solution.py:383
  40.7 1.3 %collective-permute-start.12 = (f32[16,128]{1,0:T(8,128)S(1)}, f32[16,128]{1,0:T(8,128)S(1)}, u32[]{:S(2)}, u32[]{:S(2)}) collective-permute-start(f32[16,128]{1,0:T(8,128)S(1)} %slice.7), channel_id=1, source_target_pairs={{0,4},{4,0},{8,12},{12,8},{1,5},{5,1},{9,13},{13,9},{2,6},{6,2},{1... | collective-permute-start | bytes 24584 | tf_op jit(solution)/shard_map/ppermute | solution.py:385
  41.9 0.8 %collective-permute-done.12.refs_4_ = f32[16,128]{1,0:T(8,128)S(1)} collective-permute-done((f32[16,128]{1,0:T(8,128)S(1)}, f32[16,128]{1,0:T(8,128)S(1)}, u32[]{:S(2)}, u32[]{:S(2)}) %collective-permute-start.12) | collective-permute-done | bytes 8224 | tf_op jit(solution)/shard_map/ppermute | solution.py:385
  42.8 0.2 collective-permute-done.13.refs_5_
  43.0 0.0 collective-permute-done.11.refs_3_
  43.0 1.1 %transport.1 = f32[576,128]{1,0:T(8,128)} custom-call(f32[576,128]{1,0:T(8,128)S(1)} %get-tuple-element.48.refs_0_, s32[288,128]{1,0:T(8,128)S(1)} %bitcast.11, f32[1440,128]{1,0:T(8,128)S(1)} %bitcast.7, f32[64,128]{1,0:T(8,128)S(1)} %collective-permute-done.11.refs_3_, f32[16,128]{1,0:T(8,128)S(1)} %collective-permute-done.12.refs_4_, ...), custom_call_target="tpu_custom_call" | custom-call | tf_op jit(solution)/shard_map/transport/pallas_call | solution.py:17
  (5 shorter events, 0.0 us)
Async XLA Ops:
  0.0 0.9 %copy-start.3 = (f32[72,4,128]{2,1,0:T(4,128)S(1)}, f32[72,4,128]{2,1,0:T(4,128)}, u32[]{:S(2)}) copy-start(f32[72,4,128]{2,1,0:T(4,128)} %thickness_ref.1) | copy-start | bytes 442372
  0.9 0.9 %copy-start.4 = (f32[72,4,128]{2,1,0:T(4,128)S(1)}, f32[72,4,128]{2,1,0:T(4,128)}, u32[]{:S(2)}) copy-start(f32[72,4,128]{2,1,0:T(4,128)} %diffusivity_ref.1) | copy-start | bytes 442372
  1.8 0.7 %copy-start.5 = (s32[4,128]{1,0:T(4,128)S(1)}, s32[4,128]{1,0:T(4,128)}, u32[]{:S(2)}) copy-start(s32[4,128]{1,0:T(4,128)} %counts_ref.1) | copy-start | bytes 6148
  2.5 22.9 %copy-start = (f32[5,18,16,128]{3,2,1,0:T(8,128)S(1)}, f32[5,18,16,128]{3,2,1,0:T(8,128)}, u32[]{:S(2)}) copy-start(f32[5,18,16,128]{3,2,1,0:T(8,128)} %param.8) | copy-start | bytes 2211844
  3.0 5.7 %collective-permute-start = (f32[37,4,128]{2,1,0:T(4,128)S(1)}, f32[37,4,128]{2,1,0:T(4,128)S(1)}, u32[]{:S(2)}, u32[]{:S(2)}) collective-permute-start(f32[37,4,128]{2,1,0:T(4,128)S(1)} %get-tuple-element.29), channel_id=1, source_target_pairs={{0,1},{1,0},{2,3},{3,2},{4,5},{5,4},{6,7},{7,6},{8,9},{9,8},{10,11... | collective-permute-start | bytes 227336 | tf_op jit(solution)/shard_map/ppermute | solution.py:326
  6.2 7.9 %collective-permute-start.1 = (f32[37,4,128]{2,1,0:T(4,128)S(1)}, f32[37,4,128]{2,1,0:T(4,128)S(1)}, u32[]{:S(2)}, u32[]{:S(2)}) collective-permute-start(f32[37,4,128]{2,1,0:T(4,128)S(1)} %get-tuple-element.30), channel_id=1, source_target_pairs={{0,2},{1,3},{2,0},{3,1},{4,6},{5,7},{6,4},{7,5},{8,10},{9,11},{10,... | collective-permute-start | bytes 227336 | tf_op jit(solution)/shard_map/ppermute | solution.py:326
  8.7 6.3 %collective-permute-start.2 = (f32[37,4,128]{2,1,0:T(4,128)S(1)}, f32[37,4,128]{2,1,0:T(4,128)S(1)}, u32[]{:S(2)}, u32[]{:S(2)}) collective-permute-start(f32[37,4,128]{2,1,0:T(4,128)S(1)} %get-tuple-element.31), channel_id=1, source_target_pairs={{0,3},{1,2},{2,1},{3,0},{4,7},{5,6},{6,5},{7,4},{8,11},{9,10},{10,... | collective-permute-start | bytes 227336 | tf_op jit(solution)/shard_map/ppermute | solution.py:326
  15.0 1.0 %copy-start.2 = (f32[2,18,16,128]{3,2,1,0:T(8,128)S(1)}, f32[2,18,16,128]{3,2,1,0:T(8,128)}, u32[]{:S(2)}) copy-start(f32[2,18,16,128]{3,2,1,0:T(8,128)} %param.7) | copy-start | bytes 884740
  16.0 1.6 %copy-start.6 = (s32[128]{0:T(128)S(1)}, s32[128]{0:T(128)}, u32[]{:S(2)}) copy-start(s32[128]{0:T(128)} %param.13) | copy-start | bytes 1540
  16.2 9.2 %copy-start.1 = (s32[18,16,128]{2,1,0:T(8,128)S(1)}, s32[18,16,128]{2,1,0:T(8,128)}, u32[]{:S(2)}) copy-start(s32[18,16,128]{2,1,0:T(8,128)} %param.9) | copy-start | bytes 442372
  16.3 4.3 %collective-permute-start.3 = (f32[128,128]{1,0:T(8,128)S(1)}, f32[128,128]{1,0:T(8,128)S(1)}, u32[]{:S(2)}, u32[]{:S(2)}) collective-permute-start(f32[128,128]{1,0:T(8,128)S(1)} %get-tuple-element.32.mine_ref.refs_0_.refs_2_), channel_id=1, source_target_pairs={{0,1},{1,0},{2,3},{3,2},{4,5},{5,4},{6,7},{7,6},{8,9},{9,8},{10,11... | collective-permute-start | bytes 196616 | tf_op jit(solution)/shard_map/ppermute | solution.py:326
  20.6 4.8 %collective-permute-start.4 = (f32[48,128]{1,0:T(8,128)S(1)}, f32[48,128]{1,0:T(8,128)S(1)}, u32[]{:S(2)}, u32[]{:S(2)}) collective-permute-start(f32[48,128]{1,0:T(8,128)S(1)} %get-tuple-element.33), channel_id=1, source_target_pairs={{0,2},{1,3},{2,0},{3,1},{4,6},{5,7},{6,4},{7,5},{8,10},{9,11},{10,... | collective-permute-start | bytes 73736 | tf_op jit(solution)/shard_map/ppermute | solution.py:326
  25.7 4.0 %collective-permute-start.5 = (f32[64,128]{1,0:T(8,128)S(1)}, f32[64,128]{1,0:T(8,128)S(1)}, u32[]{:S(2)}, u32[]{:S(2)}) collective-permute-start(f32[64,128]{1,0:T(8,128)S(1)} %get-tuple-element.39), channel_id=1, source_target_pairs={{0,12},{4,8},{8,4},{12,0},{1,13},{5,9},{9,5},{13,1},{2,14},{6,10},... | collective-permute-start | bytes 98312 | tf_op jit(solution)/shard_map/ppermute | solution.py:384
  25.7 3.9 %collective-permute-start.7 = (f32[48,128]{1,0:T(8,128)S(1)}, f32[48,128]{1,0:T(8,128)S(1)}, u32[]{:S(2)}, u32[]{:S(2)}) collective-permute-start(f32[48,128]{1,0:T(8,128)S(1)} %get-tuple-element.40), channel_id=1, source_target_pairs={{0,16},{16,0},{1,17},{17,1},{2,18},{18,2},{3,19},{19,3},{4,20},{20... | collective-permute-start | bytes 73736 | tf_op jit(solution)/shard_map/ppermute | solution.py:383
  27.3 2.1 %collective-permute-start.6 = (f32[16,128]{1,0:T(8,128)S(1)}, f32[16,128]{1,0:T(8,128)S(1)}, u32[]{:S(2)}, u32[]{:S(2)}) collective-permute-start(f32[16,128]{1,0:T(8,128)S(1)} %slice.6), channel_id=1, source_target_pairs={{0,4},{4,0},{8,12},{12,8},{1,5},{5,1},{9,13},{13,9},{2,6},{6,2},{1... | collective-permute-start | bytes 24584 | tf_op jit(solution)/shard_map/ppermute | solution.py:385
  30.1 8.7 %collective-permute-start.8 = (f32[64,128]{1,0:T(8,128)S(1)}, f32[64,128]{1,0:T(8,128)S(1)}, u32[]{:S(2)}, u32[]{:S(2)}) collective-permute-start(f32[64,128]{1,0:T(8,128)S(1)} %get-tuple-element.45.refs_0_), channel_id=1, source_target_pairs={{0,1},{1,0},{2,3},{3,2},{4,5},{5,4},{6,7},{7,6},{8,9},{9,8},{10,11... | collective-permute-start | bytes 98312 | tf_op jit(solution)/shard_map/ppermute | solution.py:326
  31.4 5.5 %collective-permute-start.10 = (f32[32,128]{1,0:T(8,128)S(1)}, f32[32,128]{1,0:T(8,128)S(1)}, u32[]{:S(2)}, u32[]{:S(2)}) collective-permute-start(f32[32,128]{1,0:T(8,128)S(1)} %get-tuple-element.46), channel_id=1, source_target_pairs={{0,3},{1,2},{2,1},{3,0},{4,7},{5,6},{6,5},{7,4},{8,11},{9,10},{10,... | collective-permute-start | bytes 49160 | tf_op jit(solution)/shard_map/ppermute | solution.py:326
  34.1 4.6 %collective-permute-start.9 = (f32[32,128]{1,0:T(8,128)S(1)}, f32[32,128]{1,0:T(8,128)S(1)}, u32[]{:S(2)}, u32[]{:S(2)}) collective-permute-start(f32[32,128]{1,0:T(8,128)S(1)} %get-tuple-element.46), channel_id=1, source_target_pairs={{0,2},{1,3},{2,0},{3,1},{4,6},{5,7},{6,4},{7,5},{8,10},{9,11},{10,... | collective-permute-start | bytes 49160 | tf_op jit(solution)/shard_map/ppermute | solution.py:326
  39.0 4.0 %collective-permute-start.11 = (f32[64,128]{1,0:T(8,128)S(1)}, f32[64,128]{1,0:T(8,128)S(1)}, u32[]{:S(2)}, u32[]{:S(2)}) collective-permute-start(f32[64,128]{1,0:T(8,128)S(1)} %get-tuple-element.49), channel_id=1, source_target_pairs={{0,12},{4,8},{8,4},{12,0},{1,13},{5,9},{9,5},{13,1},{2,14},{6,10},... | collective-permute-start | bytes 98312 | tf_op jit(solution)/shard_map/ppermute | solution.py:384
  39.1 3.9 %collective-permute-start.13 = (f32[48,128]{1,0:T(8,128)S(1)}, f32[48,128]{1,0:T(8,128)S(1)}, u32[]{:S(2)}, u32[]{:S(2)}) collective-permute-start(f32[48,128]{1,0:T(8,128)S(1)} %get-tuple-element.50), channel_id=1, source_target_pairs={{0,16},{16,0},{1,17},{17,1},{2,18},{18,2},{3,19},{19,3},{4,20},{20... | collective-permute-start | bytes 73736 | tf_op jit(solution)/shard_map/ppermute | solution.py:383
  40.7 2.1 %collective-permute-start.12 = (f32[16,128]{1,0:T(8,128)S(1)}, f32[16,128]{1,0:T(8,128)S(1)}, u32[]{:S(2)}, u32[]{:S(2)}) collective-permute-start(f32[16,128]{1,0:T(8,128)S(1)} %slice.7), channel_id=1, source_target_pairs={{0,4},{4,0},{8,12},{12,8},{1,5},{5,1},{9,13},{13,9},{2,6},{6,2},{1... | collective-permute-start | bytes 24584 | tf_op jit(solution)/shard_map/ppermute | solution.py:385

commit v2 on v1

--- a/solution.py
+++ b/solution.py
@@ -7,31 +7,31 @@
 from jax.experimental.pallas import tpu as pltpu
 from jax.sharding import PartitionSpec as P
 
+
 STEPS = 2
 TRACERS = 2
 GRANT = 12 * 2**20
 
 
-def call(kernel, name, out_shapes, operands, scratch=(), copies=0, read_in_place=False, write_in_place=False):
-    vmem, any_space = pl.BlockSpec(memory_space=pltpu.VMEM), pl.BlockSpec(memory_space=pl.ANY)
+def call(kernel, out_shapes, operands, scratch=(), copies=0, read_in_place=False, write_in_place=False):
+    vmem, any_space = pl.BlockSpec(memory_space=pltpu.VMEM), pl.BlockSpec(memory_space=pltpu.HBM)
     return pl.pallas_call(
         kernel,
-        name=name,
         out_shape=[jax.ShapeDtypeStruct(shape, jnp.float32) for shape in out_shapes],
         in_specs=[any_space if read_in_place else vmem] * len(operands),
         out_specs=[any_space if write_in_place else vmem] * len(out_shapes),
         scratch_shapes=[pltpu.VMEM(*shape) if isinstance(shape[0], tuple) else pltpu.VMEM(shape, jnp.float32) for shape in scratch]
         + [pltpu.SemaphoreType.DMA((copies,))] * (copies > 0),
         compiler_params=pltpu.CompilerParams(vmem_limit_bytes=GRANT),
-    )(*operands)
+    )(*((pltpu.with_memory_space_constraint(x, pltpu.HBM) for x in operands) if read_in_place else operands))
 
 
 def span(ref, index, rows):
     return ref[pl.ds(index * rows, rows), :]
 
 
-def pack_kernel(levels, places, thickness_ref, diffusivity_ref, counts_ref, *refs):
-    out_refs, (held_ref, held_counts_ref, sems) = refs[:places], refs[places:]
+def pack_kernel(levels, places, thickness_ref, diffusivity_ref, counts_ref, adj_ref, *refs):
+    out_refs, (near_adj_ref, held_ref, held_counts_ref, sems) = refs[:places], refs[places:]
     me = lax.axis_index("lev")
     ahead = [
         pltpu.make_async_copy(counts_ref, held_counts_ref, sems.at[0]),
@@ -40,6 +40,7 @@
     for distance in range(places):
         source = thickness_ref.at[pl.ds((me ^ distance) * levels, levels)]
         ahead.append(pltpu.make_async_copy(source, out_refs[distance].at[pl.ds(0, levels)], sems.at[2 + distance]))
+    ahead.append(pltpu.make_async_copy(adj_ref, near_adj_ref, sems.at[2 + places]))
     for copy in ahead:
         copy.start()
     for copy in ahead[:2]:
@@ -333,13 +334,12 @@
     lat_near = [(i, i ^ 1) for i in range(lat_count)]
     lat_wide = [pair for i in range(1, lat_count - 1, 2) for pair in ((i, i + 1), (i + 1, i))]
 
-    own, *parts = call(
+    own, *parts, near_adj = call(
         functools.partial(pack_kernel, levels, places),
-        "pack_columns",
-        [(2 * levels + 1, strip, width)] * places,
-        (thickness, diffusivity, level_counts),
+        [(2 * levels + 1, strip, width)] * places + [flat],
+        (thickness, diffusivity, level_counts, adj),
         [thickness.shape, (level_counts.shape, jnp.int32)],
-        2 + places,
+        3 + places,
         read_in_place=True,
     )
     parts = [lev_swap(parts[distance - 1], distance) for distance in range(places - 1, 0, -1)][::-1]
@@ -352,19 +352,15 @@
 
     solved, ends, rp, a, c, t, tv, tw = call(
         functools.partial(first_kernel, levels, places, strip),
-        "first_solve",
         [flat, (8 * rows, width)] + [column] * 6,
-        (*parts, adj),
+        (*parts, near_adj),
         [((levels + 1) * rows, width)],
     )
     for turn_index in range(STEPS):
         if turn_index == 0:
             other = lev_swap(ends, 1)
             near, share = call(
-                functools.partial(merge_kernel, rows),
-                "merge_pair",
-                [((TRACERS + 1) * rows, width), (2 * rows, width)],
-                (ends, other),
+                functools.partial(merge_kernel, rows), [((TRACERS + 1) * rows, width), (2 * rows, width)], (ends, other)
             )
             far = more = far_beta = lev_swap(near, 2)
             spikes, other_spikes = ends, other
@@ -375,7 +371,6 @@
         messages += [(48, width)] * (lat_two_ways + fold_apart)
         vertical, lon_message, lat_message, *rest = call(
             functools.partial(finish_kernel, levels, rows, lat_two_ways, fold_apart, turn_index > 0),
-            "finish_solve",
             [flat] + messages,
             (ends, other, spikes, other_spikes, far, more, far_beta, solved, t, tv, tw, mask, weights, source),
             [flat, (48, width)],
@@ -393,7 +388,6 @@
         if turn_index < STEPS - 1:
             solved, ends, alpha = call(
                 functools.partial(turn_kernel, levels, rows, lat_two_ways, fold_apart),
-                "transport_and_solve",
                 [flat, (4 * rows, width), (2 * rows, width)],
                 (*operands, rp, a, c, share),
                 [pad],
@@ -401,7 +395,6 @@
         else:
             out = call(
                 functools.partial(last_kernel, levels, rows, lat_two_ways, fold_apart),
-                "transport",
                 [flat],
                 operands,
                 [pad, flat],

time: 44.3 us -> 41.5 us (0.937)
  local copies, waits for them, and re-layouts: 3.48 us -> 0.02 us
  Pallas kernels: 2.81 us -> 3.55 us
    unnamed x14 -> x6, local copies, waits for them, and re-layouts: 3.48 us -> 0.01 us
    pallas_call x7, Pallas kernels: 2.81 us -> 3.55 us  [call(): pl.pallas_call(kernel, out_shape=[jax.ShapeDtypeStruct(shape, jnp.float32...]
where the time goes in v2:
time: 41.5 us; the launch traced here: 41.3 us
  starting transfers between devices  19.4 us (47%)
  waiting for transfers between devices  18.2 us (44%)
  Pallas kernels  3.55 us (9%)
    ppermute x8, waiting for transfers between devices, lev_swap(): lax.ppermute(value, 'lev', [(i, i ^ distance) for i in range(places)])  16 us
    ppermute x8, starting transfers between devices, lev_swap(): lax.ppermute(value, 'lev', [(i, i ^ distance) for i in range(places)])  13.6 us
    pallas_call x7, Pallas kernels, call(): pl.pallas_call(kernel, out_shape=[jax.ShapeDtypeStruct(shape, jnp.float32...  3.55 us
    ppermute x2, starting transfers between devices, shards(): from_lat = lax.ppermute(lat_message, 'lat', lat_near)  3.11 us
    ppermute x2, starting transfers between devices, shards(): from_near = lax.ppermute(lon_message[:rows], 'lon', near_pairs)  2.55 us
    ppermute x2, waiting for transfers between devices, shards(): from_near = lax.ppermute(lon_message[:rows], 'lon', near_pairs)  1.66 us
  transfers between devices with their start and end apart: 14, of which 10 were waited for; matrix products, arithmetic and copies ran while one was open for 0% of the time, Pallas kernels for 0%

profile of v2, /device:TPU:0, one launch (start us, length us, event | category | flops | bytes accessed | tf_op | source)
XLA Modules:
  0.0 41.3 jit_solution(14368845437759958166)
XLA Ops:
  0.0 0.0 copy-start
  0.0 1.2 %shard_map.73 = (f32[37,4,128]{2,1,0:T(4,128)S(1)}, f32[37,4,128]{2,1,0:T(4,128)S(1)}, f32[37,4,128]{2,1,0:T(4,128)S(1)}, f32[37,4,128]{2,1,0:T(4,128)S(1)}, f32[576,128]{1,0:T(8,128)S(1)}) custom-call(f32[72,4,128]{2,1,0:T(4,128)} %thickness_ref.1, f32[72,4,128]{2,1,0:T(4,128)} %diffusivity_ref.1, s32[4,128]{1,0:T(4,128)} %counts_ref.1, f32[576,128]{1,0:T(8,128)} %bitcast.12), custom_call_target="tpu_custom_call" | custom-call | tf_op jit(solution)/shard_map/pallas_call | solution.py:18
  1.3 3.1 %collective-permute-start = (f32[37,4,128]{2,1,0:T(4,128)S(1)}, f32[37,4,128]{2,1,0:T(4,128)S(1)}, u32[]{:S(2)}, u32[]{:S(2)}) collective-permute-start(f32[37,4,128]{2,1,0:T(4,128)S(1)} %get-tuple-element.30), channel_id=1, source_target_pairs={{0,1},{1,0},{2,3},{3,2},{4,5},{5,4},{6,7},{7,6},{8,9},{9,8},{10,11... | collective-permute-start | bytes 227336 | tf_op jit(solution)/shard_map/ppermute | solution.py:327
  4.4 2.6 %collective-permute-start.1 = (f32[37,4,128]{2,1,0:T(4,128)S(1)}, f32[37,4,128]{2,1,0:T(4,128)S(1)}, u32[]{:S(2)}, u32[]{:S(2)}) collective-permute-start(f32[37,4,128]{2,1,0:T(4,128)S(1)} %get-tuple-element.31), channel_id=1, source_target_pairs={{0,2},{1,3},{2,0},{3,1},{4,6},{5,7},{6,4},{7,5},{8,10},{9,11},{10,... | collective-permute-start | bytes 227336 | tf_op jit(solution)/shard_map/ppermute | solution.py:327
  7.0 0.0 collective-permute-start.2
  7.0 0.0 collective-permute-done.refs_1_
  7.0 5.3 %collective-permute-done.1.refs_2_ = f32[37,4,128]{2,1,0:T(4,128)S(1)} collective-permute-done((f32[37,4,128]{2,1,0:T(4,128)S(1)}, f32[37,4,128]{2,1,0:T(4,128)S(1)}, u32[]{:S(2)}, u32[]{:S(2)}) %collective-permute-start.1) | collective-permute-done | bytes 75808 | tf_op jit(solution)/shard_map/ppermute | solution.py:327
  12.3 0.9 %collective-permute-done.2.refs_3_ = f32[37,4,128]{2,1,0:T(4,128)S(1)} collective-permute-done((f32[37,4,128]{2,1,0:T(4,128)S(1)}, f32[37,4,128]{2,1,0:T(4,128)S(1)}, u32[]{:S(2)}, u32[]{:S(2)}) %collective-permute-start.2) | collective-permute-done | bytes 75808 | tf_op jit(solution)/shard_map/ppermute | solution.py:327
  13.2 0.0 copy-start.2
  13.2 0.3 shard_map.74
  13.5 0.0 copy-start.1
  13.5 1.3 %collective-permute-start.3 = (f32[128,128]{1,0:T(8,128)S(1)}, f32[128,128]{1,0:T(8,128)S(1)}, u32[]{:S(2)}, u32[]{:S(2)}) collective-permute-start(f32[128,128]{1,0:T(8,128)S(1)} %get-tuple-element.34.mine_ref.refs_0_.refs_2_), channel_id=1, source_target_pairs={{0,1},{1,0},{2,3},{3,2},{4,5},{5,4},{6,7},{7,6},{8,9},{9,8},{10,11... | collective-permute-start | bytes 196616 | tf_op jit(solution)/shard_map/ppermute | solution.py:327
  14.8 0.0 copy-done.2
  14.8 3.0 %collective-permute-done.3.other_ref.refs_1_.refs_3_ = f32[128,128]{1,0:T(8,128)S(1)} collective-permute-done((f32[128,128]{1,0:T(8,128)S(1)}, f32[128,128]{1,0:T(8,128)S(1)}, u32[]{:S(2)}, u32[]{:S(2)}) %collective-permute-start.3) | collective-permute-done | bytes 65568 | tf_op jit(solution)/shard_map/ppermute | solution.py:327
  17.9 2.6 %collective-permute-start.4 = (f32[48,128]{1,0:T(8,128)S(1)}, f32[48,128]{1,0:T(8,128)S(1)}, u32[]{:S(2)}, u32[]{:S(2)}) collective-permute-start(f32[48,128]{1,0:T(8,128)S(1)} %get-tuple-element.35), channel_id=1, source_target_pairs={{0,2},{1,3},{2,0},{3,1},{4,6},{5,7},{6,4},{7,5},{8,10},{9,11},{10,... | collective-permute-start | bytes 73736 | tf_op jit(solution)/shard_map/ppermute | solution.py:327
  20.5 0.1 select_reduce_fusion
  20.6 2.1 %collective-permute-done.4.refs_4_.refs_5_.refs_6_ = f32[48,128]{1,0:T(8,128)S(1)} collective-permute-done((f32[48,128]{1,0:T(8,128)S(1)}, f32[48,128]{1,0:T(8,128)S(1)}, u32[]{:S(2)}, u32[]{:S(2)}) %collective-permute-start.4) | collective-permute-done | bytes 24608 | tf_op jit(solution)/shard_map/ppermute | solution.py:327
  22.7 0.0 copy-done
  22.7 0.0 copy-done.1
  22.7 0.2 shard_map.76
  22.9 0.1 collective-permute-start.5
  23.0 1.6 %collective-permute-start.7 = (f32[48,128]{1,0:T(8,128)S(1)}, f32[48,128]{1,0:T(8,128)S(1)}, u32[]{:S(2)}, u32[]{:S(2)}) collective-permute-start(f32[48,128]{1,0:T(8,128)S(1)} %get-tuple-element.42), channel_id=1, source_target_pairs={{0,16},{16,0},{1,17},{17,1},{2,18},{18,2},{3,19},{19,3},{4,20},{20... | collective-permute-start | bytes 73736 | tf_op jit(solution)/shard_map/ppermute | solution.py:378
  24.6 1.3 %collective-permute-start.6 = (f32[16,128]{1,0:T(8,128)S(1)}, f32[16,128]{1,0:T(8,128)S(1)}, u32[]{:S(2)}, u32[]{:S(2)}) collective-permute-start(f32[16,128]{1,0:T(8,128)S(1)} %slice.6), channel_id=1, source_target_pairs={{0,4},{4,0},{8,12},{12,8},{1,5},{5,1},{9,13},{13,9},{2,6},{6,2},{1... | collective-permute-start | bytes 24584 | tf_op jit(solution)/shard_map/ppermute | solution.py:380
  25.8 0.8 %collective-permute-done.6.refs_4_ = f32[16,128]{1,0:T(8,128)S(1)} collective-permute-done((f32[16,128]{1,0:T(8,128)S(1)}, f32[16,128]{1,0:T(8,128)S(1)}, u32[]{:S(2)}, u32[]{:S(2)}) %collective-permute-start.6) | collective-permute-done | bytes 8224 | tf_op jit(solution)/shard_map/ppermute | solution.py:380
  26.7 0.2 collective-permute-done.7.refs_5_
  26.9 0.0 collective-permute-done.5.refs_3_
  26.9 0.5 %shard_map.77 = (f32[576,128]{1,0:T(8,128)S(1)}, f32[64,128]{1,0:T(8,128)S(1)}, f32[32,128]{1,0:T(8,128)S(1)}) custom-call(f32[576,128]{1,0:T(8,128)S(1)} %get-tuple-element.40.refs_0_, s32[288,128]{1,0:T(8,128)S(1)} %bitcast.9, f32[1440,128]{1,0:T(8,128)S(1)} %bitcast.5, f32[64,128]{1,0:T(8,128)S(1)} %collective-permute-done.5.refs_3_, ...), custom_call_target="tpu_custom_call" | custom-call | tf_op jit(solution)/shard_map/pallas_call | solution.py:18
  27.4 1.3 %collective-permute-start.8 = (f32[64,128]{1,0:T(8,128)S(1)}, f32[64,128]{1,0:T(8,128)S(1)}, u32[]{:S(2)}, u32[]{:S(2)}) collective-permute-start(f32[64,128]{1,0:T(8,128)S(1)} %get-tuple-element.47.refs_0_), channel_id=1, source_target_pairs={{0,1},{1,0},{2,3},{3,2},{4,5},{5,4},{6,7},{7,6},{8,9},{9,8},{10,11... | collective-permute-start | bytes 98312 | tf_op jit(solution)/shard_map/ppermute | solution.py:327
  28.7 2.7 %collective-permute-start.10 = (f32[32,128]{1,0:T(8,128)S(1)}, f32[32,128]{1,0:T(8,128)S(1)}, u32[]{:S(2)}, u32[]{:S(2)}) collective-permute-start(f32[32,128]{1,0:T(8,128)S(1)} %get-tuple-element.48), channel_id=1, source_target_pairs={{0,3},{1,2},{2,1},{3,0},{4,7},{5,6},{6,5},{7,4},{8,11},{9,10},{10,... | collective-permute-start | bytes 49160 | tf_op jit(solution)/shard_map/ppermute | solution.py:327
  31.4 0.0 collective-permute-start.9
  31.4 2.8 %collective-permute-done.10.refs_5_ = f32[32,128]{1,0:T(8,128)S(1)} collective-permute-done((f32[32,128]{1,0:T(8,128)S(1)}, f32[32,128]{1,0:T(8,128)S(1)}, u32[]{:S(2)}, u32[]{:S(2)}) %collective-permute-start.10) | collective-permute-done | bytes 16416 | tf_op jit(solution)/shard_map/ppermute | solution.py:327
  34.2 1.8 %collective-permute-done.9.refs_4_ = f32[32,128]{1,0:T(8,128)S(1)} collective-permute-done((f32[32,128]{1,0:T(8,128)S(1)}, f32[32,128]{1,0:T(8,128)S(1)}, u32[]{:S(2)}, u32[]{:S(2)}) %collective-permute-start.9) | collective-permute-done | bytes 16416 | tf_op jit(solution)/shard_map/ppermute | solution.py:327
  36.0 0.0 collective-permute-done.8.refs_1_
  36.0 0.2 shard_map.78
  36.3 0.1 collective-permute-start.11
  36.4 1.6 %collective-permute-start.13 = (f32[48,128]{1,0:T(8,128)S(1)}, f32[48,128]{1,0:T(8,128)S(1)}, u32[]{:S(2)}, u32[]{:S(2)}) collective-permute-start(f32[48,128]{1,0:T(8,128)S(1)} %get-tuple-element.52), channel_id=1, source_target_pairs={{0,16},{16,0},{1,17},{17,1},{2,18},{18,2},{3,19},{19,3},{4,20},{20... | collective-permute-start | bytes 73736 | tf_op jit(solution)/shard_map/ppermute | solution.py:378
  37.9 1.3 %collective-permute-start.12 = (f32[16,128]{1,0:T(8,128)S(1)}, f32[16,128]{1,0:T(8,128)S(1)}, u32[]{:S(2)}, u32[]{:S(2)}) collective-permute-start(f32[16,128]{1,0:T(8,128)S(1)} %slice.7), channel_id=1, source_target_pairs={{0,4},{4,0},{8,12},{12,8},{1,5},{5,1},{9,13},{13,9},{2,6},{6,2},{1... | collective-permute-start | bytes 24584 | tf_op jit(solution)/shard_map/ppermute | solution.py:380
  39.2 0.8 %collective-permute-done.12.refs_4_ = f32[16,128]{1,0:T(8,128)S(1)} collective-permute-done((f32[16,128]{1,0:T(8,128)S(1)}, f32[16,128]{1,0:T(8,128)S(1)}, u32[]{:S(2)}, u32[]{:S(2)}) %collective-permute-start.12) | collective-permute-done | bytes 8224 | tf_op jit(solution)/shard_map/ppermute | solution.py:380
  40.0 0.2 collective-permute-done.13.refs_5_
  40.3 0.0 collective-permute-done.11.refs_3_
  40.3 1.1 %shard_map.79 = f32[576,128]{1,0:T(8,128)} custom-call(f32[576,128]{1,0:T(8,128)S(1)} %get-tuple-element.50.refs_0_, s32[288,128]{1,0:T(8,128)S(1)} %bitcast.11, f32[1440,128]{1,0:T(8,128)S(1)} %bitcast.7, f32[64,128]{1,0:T(8,128)S(1)} %collective-permute-done.11.refs_3_, f32[16,128]{1,0:T(8,128)S(1)} %collective-permute-done.12.refs_4_, ...), custom_call_target="tpu_custom_call" | custom-call | tf_op jit(solution)/shard_map/pallas_call | solution.py:18
  (5 shorter events, 0.0 us)
Async XLA Ops:
  0.0 22.7 %copy-start = (f32[5,18,16,128]{3,2,1,0:T(8,128)S(1)}, f32[5,18,16,128]{3,2,1,0:T(8,128)}, u32[]{:S(2)}) copy-start(f32[5,18,16,128]{3,2,1,0:T(8,128)} %param.8) | copy-start | bytes 2211844
  1.3 5.7 %collective-permute-start = (f32[37,4,128]{2,1,0:T(4,128)S(1)}, f32[37,4,128]{2,1,0:T(4,128)S(1)}, u32[]{:S(2)}, u32[]{:S(2)}) collective-permute-start(f32[37,4,128]{2,1,0:T(4,128)S(1)} %get-tuple-element.30), channel_id=1, source_target_pairs={{0,1},{1,0},{2,3},{3,2},{4,5},{5,4},{6,7},{7,6},{8,9},{9,8},{10,11... | collective-permute-start | bytes 227336 | tf_op jit(solution)/shard_map/ppermute | solution.py:327
  4.4 7.9 %collective-permute-start.1 = (f32[37,4,128]{2,1,0:T(4,128)S(1)}, f32[37,4,128]{2,1,0:T(4,128)S(1)}, u32[]{:S(2)}, u32[]{:S(2)}) collective-permute-start(f32[37,4,128]{2,1,0:T(4,128)S(1)} %get-tuple-element.31), channel_id=1, source_target_pairs={{0,2},{1,3},{2,0},{3,1},{4,6},{5,7},{6,4},{7,5},{8,10},{9,11},{10,... | collective-permute-start | bytes 227336 | tf_op jit(solution)/shard_map/ppermute | solution.py:327
  7.0 6.3 %collective-permute-start.2 = (f32[37,4,128]{2,1,0:T(4,128)S(1)}, f32[37,4,128]{2,1,0:T(4,128)S(1)}, u32[]{:S(2)}, u32[]{:S(2)}) collective-permute-start(f32[37,4,128]{2,1,0:T(4,128)S(1)} %get-tuple-element.32), channel_id=1, source_target_pairs={{0,3},{1,2},{2,1},{3,0},{4,7},{5,6},{6,5},{7,4},{8,11},{9,10},{10,... | collective-permute-start | bytes 227336 | tf_op jit(solution)/shard_map/ppermute | solution.py:327
  13.2 1.6 %copy-start.2 = (s32[128]{0:T(128)S(1)}, s32[128]{0:T(128)}, u32[]{:S(2)}) copy-start(s32[128]{0:T(128)} %param.13) | copy-start | bytes 1540
  13.5 9.2 %copy-start.1 = (s32[18,16,128]{2,1,0:T(8,128)S(1)}, s32[18,16,128]{2,1,0:T(8,128)}, u32[]{:S(2)}) copy-start(s32[18,16,128]{2,1,0:T(8,128)} %param.9) | copy-start | bytes 442372
  13.5 4.3 %collective-permute-start.3 = (f32[128,128]{1,0:T(8,128)S(1)}, f32[128,128]{1,0:T(8,128)S(1)}, u32[]{:S(2)}, u32[]{:S(2)}) collective-permute-start(f32[128,128]{1,0:T(8,128)S(1)} %get-tuple-element.34.mine_ref.refs_0_.refs_2_), channel_id=1, source_target_pairs={{0,1},{1,0},{2,3},{3,2},{4,5},{5,4},{6,7},{7,6},{8,9},{9,8},{10,11... | collective-permute-start | bytes 196616 | tf_op jit(solution)/shard_map/ppermute | solution.py:327
  17.9 4.8 %collective-permute-start.4 = (f32[48,128]{1,0:T(8,128)S(1)}, f32[48,128]{1,0:T(8,128)S(1)}, u32[]{:S(2)}, u32[]{:S(2)}) collective-permute-start(f32[48,128]{1,0:T(8,128)S(1)} %get-tuple-element.35), channel_id=1, source_target_pairs={{0,2},{1,3},{2,0},{3,1},{4,6},{5,7},{6,4},{7,5},{8,10},{9,11},{10,... | collective-permute-start | bytes 73736 | tf_op jit(solution)/shard_map/ppermute | solution.py:327
  22.9 4.0 %collective-permute-start.5 = (f32[64,128]{1,0:T(8,128)S(1)}, f32[64,128]{1,0:T(8,128)S(1)}, u32[]{:S(2)}, u32[]{:S(2)}) collective-permute-start(f32[64,128]{1,0:T(8,128)S(1)} %get-tuple-element.41), channel_id=1, source_target_pairs={{0,12},{4,8},{8,4},{12,0},{1,13},{5,9},{9,5},{13,1},{2,14},{6,10},... | collective-permute-start | bytes 98312 | tf_op jit(solution)/shard_map/ppermute | solution.py:379
  23.0 3.9 %collective-permute-start.7 = (f32[48,128]{1,0:T(8,128)S(1)}, f32[48,128]{1,0:T(8,128)S(1)}, u32[]{:S(2)}, u32[]{:S(2)}) collective-permute-start(f32[48,128]{1,0:T(8,128)S(1)} %get-tuple-element.42), channel_id=1, source_target_pairs={{0,16},{16,0},{1,17},{17,1},{2,18},{18,2},{3,19},{19,3},{4,20},{20... | collective-permute-start | bytes 73736 | tf_op jit(solution)/shard_map/ppermute | solution.py:378
  24.6 2.1 %collective-permute-start.6 = (f32[16,128]{1,0:T(8,128)S(1)}, f32[16,128]{1,0:T(8,128)S(1)}, u32[]{:S(2)}, u32[]{:S(2)}) collective-permute-start(f32[16,128]{1,0:T(8,128)S(1)} %slice.6), channel_id=1, source_target_pairs={{0,4},{4,0},{8,12},{12,8},{1,5},{5,1},{9,13},{13,9},{2,6},{6,2},{1... | collective-permute-start | bytes 24584 | tf_op jit(solution)/shard_map/ppermute | solution.py:380
  27.4 8.7 %collective-permute-start.8 = (f32[64,128]{1,0:T(8,128)S(1)}, f32[64,128]{1,0:T(8,128)S(1)}, u32[]{:S(2)}, u32[]{:S(2)}) collective-permute-start(f32[64,128]{1,0:T(8,128)S(1)} %get-tuple-element.47.refs_0_), channel_id=1, source_target_pairs={{0,1},{1,0},{2,3},{3,2},{4,5},{5,4},{6,7},{7,6},{8,9},{9,8},{10,11... | collective-permute-start | bytes 98312 | tf_op jit(solution)/shard_map/ppermute | solution.py:327
  28.7 5.5 %collective-permute-start.10 = (f32[32,128]{1,0:T(8,128)S(1)}, f32[32,128]{1,0:T(8,128)S(1)}, u32[]{:S(2)}, u32[]{:S(2)}) collective-permute-start(f32[32,128]{1,0:T(8,128)S(1)} %get-tuple-element.48), channel_id=1, source_target_pairs={{0,3},{1,2},{2,1},{3,0},{4,7},{5,6},{6,5},{7,4},{8,11},{9,10},{10,... | collective-permute-start | bytes 49160 | tf_op jit(solution)/shard_map/ppermute | solution.py:327
  31.4 4.6 %collective-permute-start.9 = (f32[32,128]{1,0:T(8,128)S(1)}, f32[32,128]{1,0:T(8,128)S(1)}, u32[]{:S(2)}, u32[]{:S(2)}) collective-permute-start(f32[32,128]{1,0:T(8,128)S(1)} %get-tuple-element.48), channel_id=1, source_target_pairs={{0,2},{1,3},{2,0},{3,1},{4,6},{5,7},{6,4},{7,5},{8,10},{9,11},{10,... | collective-permute-start | bytes 49160 | tf_op jit(solution)/shard_map/ppermute | solution.py:327
  36.3 4.0 %collective-permute-start.11 = (f32[64,128]{1,0:T(8,128)S(1)}, f32[64,128]{1,0:T(8,128)S(1)}, u32[]{:S(2)}, u32[]{:S(2)}) collective-permute-start(f32[64,128]{1,0:T(8,128)S(1)} %get-tuple-element.51), channel_id=1, source_target_pairs={{0,12},{4,8},{8,4},{12,0},{1,13},{5,9},{9,5},{13,1},{2,14},{6,10},... | collective-permute-start | bytes 98312 | tf_op jit(solution)/shard_map/ppermute | solution.py:379
  36.4 3.9 %collective-permute-start.13 = (f32[48,128]{1,0:T(8,128)S(1)}, f32[48,128]{1,0:T(8,128)S(1)}, u32[]{:S(2)}, u32[]{:S(2)}) collective-permute-start(f32[48,128]{1,0:T(8,128)S(1)} %get-tuple-element.52), channel_id=1, source_target_pairs={{0,16},{16,0},{1,17},{17,1},{2,18},{18,2},{3,19},{19,3},{4,20},{20... | collective-permute-start | bytes 73736 | tf_op jit(solution)/shard_map/ppermute | solution.py:378
  37.9 2.1 %collective-permute-start.12 = (f32[16,128]{1,0:T(8,128)S(1)}, f32[16,128]{1,0:T(8,128)S(1)}, u32[]{:S(2)}, u32[]{:S(2)}) collective-permute-start(f32[16,128]{1,0:T(8,128)S(1)} %slice.7), channel_id=1, source_target_pairs={{0,4},{4,0},{8,12},{12,8},{1,5},{5,1},{9,13},{13,9},{2,6},{6,2},{1... | collective-permute-start | bytes 24584 | tf_op jit(solution)/shard_map/ppermute | solution.py:380

commit v3 on v2

--- a/solution.py
+++ b/solution.py
@@ -172,13 +172,39 @@
         share_ref[pl.ds(i * rows, rows), :] = jnp.where(odd, share_q[i], share_p[i])
 
 
-def finish_kernel(levels, rows, lat_two_ways, fold_apart, two_shares, *refs):
+def edges_kernel(levels, rows, u_ref, t_ref, tv_ref, tw_ref, mask_ref, pack_ref, line_ref, held_ref):
+    lane = lax.broadcasted_iota(jnp.int32, (rows, 128), 1)
+    for part, source in enumerate((u_ref, tv_ref, tw_ref)):
+        packed = jnp.zeros((rows, 128), jnp.float32)
+        count = levels * (TRACERS if part == 0 else 1)
+        for j in range(count):
+            k = j % levels
+            value = span(mask_ref, k, rows).astype(jnp.float32) * span(source, j, rows)
+            if part == 0:
+                value = value * span(t_ref, k, rows)
+            held_ref[pl.ds(j * rows, rows), :] = value
+            packed = jnp.where((lane >> 1) == j, pltpu.roll(value, 2 * j + 1, 1), packed)
+        if part:
+            for tracer in range(1, TRACERS):
+                packed = jnp.where(
+                    (lane >> 1) >= tracer * levels, pltpu.roll(packed, 2 * levels, 1), packed
+                )
+        pack_ref[pl.ds(part * rows, rows), :] = packed
+        for side in range(2):
+            for tracer in range(TRACERS):
+                first = (tracer if part == 0 else 0) * levels * rows + side * (rows - 1)
+                line_ref[pl.ds((part * 2 + side) * 48 + tracer * 24, levels), :] = held_ref[
+                    pl.ds(first, levels, stride=rows), :
+                ]
+
+
+def send_kernel(levels, rows, lat_two_ways, fold_apart, two_shares, *refs):
     (
         mine_ref, other_ref, spikes_ref, other_spikes_ref, far_ref, more_ref, far_beta_ref,
-        u_ref, t_ref, tv_ref, tw_ref, mask_ref, stencil_ref, source_ref,
-    ) = refs[:14]
-    out_refs, (masked_ref, fold_ref) = refs[14:-2], refs[-2:]
-    vertical_ref, lon_ref, lat_ref = out_refs[:3]
+        pack_ref, line_ref, stencil_ref, source_ref,
+    ) = refs[:11]
+    out_refs, fold_ref = refs[11:-1], refs[-1]
+    outer_ref, lon_ref, lat_ref = out_refs[:3]
     me = lax.axis_index("lev")
     odd = (me & 1) == 1
     is_upper = me < 2
@@ -191,7 +217,10 @@
     far_det = 1.0 / (1.0 - beta * far_beta)
     zero = jnp.zeros_like(det)
     lane = lax.broadcasted_iota(jnp.int32, (rows, 128), 1)
-    packed = zero
+    lat_odd = (lax.axis_index("lat") & 1) == 1
+    weight = stencil_ref[pl.ds(3 * levels * rows + rows - 1, levels, stride=rows), :]
+    fold_ref[...] = jnp.zeros_like(fold_ref)
+    sides = []
     for tracer in range(TRACERS):
         far = span(far_ref, tracer, rows)
         if two_shares:
@@ -203,30 +232,36 @@
         first_q = q[tracer] + wf_q * below
         previous = jnp.where(odd, (last_p + wl_p * first_q) * det, above)
         following = jnp.where(odd, below, (first_q + vf_q * last_p) * det)
-        for k in range(levels):
-            j = tracer * levels + k
-            at = pl.ds(j * rows, rows)
-            vertical = (
-                span(t_ref, k, rows) * span(u_ref, j, rows)
-                + span(tv_ref, k, rows) * previous
-                + span(tw_ref, k, rows) * following
+        outer_ref[pl.ds(tracer * rows, rows), :] = previous
+        outer_ref[pl.ds((TRACERS + tracer) * rows, rows), :] = following
+        ends = []
+        for value in (previous, following):
+            west = jnp.broadcast_to(value[:, 0:1], (rows, 128))
+            east = jnp.broadcast_to(value[:, 127:128], (rows, 128))
+            ends.append(jnp.where((lane & 1) == 0, east, west))
+        sides.append(ends)
+        lines = []
+        for side, row in ((0, 0), (1, rows - 1)):
+            at = [pl.ds((part * 2 + side) * 48 + tracer * 24, levels) for part in range(3)]
+            lines.append(
+                line_ref[at[0], :]
+                + line_ref[at[1], :] * previous[row : row + 1, :]
+                + line_ref[at[2], :] * following[row : row + 1, :]
             )
-            vertical_ref[at, :] = vertical
-            masked = span(mask_ref, k, rows).astype(jnp.float32) * vertical
-            masked_ref[at, :] = masked
-            packed = jnp.where((lane >> 1) == j, pltpu.roll(masked, 2 * j + 1, 1), packed)
-    lon_ref[pl.ds(0, rows), :] = packed
-    lat_odd = (lax.axis_index("lat") & 1) == 1
-    fold_ref[...] = jnp.zeros_like(fold_ref)
-    weight = stencil_ref[pl.ds(3 * levels * rows + rows - 1, levels, stride=rows), :]
-    for tracer in range(TRACERS):
-        first = masked_ref[pl.ds(tracer * levels * rows, levels, stride=rows), :]
-        last = masked_ref[pl.ds(tracer * levels * rows + rows - 1, levels, stride=rows), :]
+        first, last = lines
         at = pl.ds(tracer * 24, levels)
         lat_ref[at, :] = jnp.where(lat_odd, first, last)
         if lat_two_ways:
             out_refs[3][at, :] = jnp.where(lat_odd, last, first)
         fold_ref[at, :] = weight * last
+    previous, following = sides[0]
+    for tracer in range(1, TRACERS):
+        later = (lane >> 1) >= tracer * levels
+        previous = jnp.where(later, sides[tracer][0], previous)
+        following = jnp.where(later, sides[tracer][1], following)
+    lon_ref[pl.ds(0, rows), :] = (
+        span(pack_ref, 0, rows) + span(pack_ref, 1, rows) * previous + span(pack_ref, 2, rows) * following
+    )
     source = source_ref[...]
     for i in range(TRACERS * 3):
         moved = jnp.take_along_axis(fold_ref[pl.ds(i * 8, 8), :], source, axis=1)
@@ -236,9 +271,45 @@
             lon_ref[pl.ds(rows + i * 8, 8), :] = moved
 
 
-def tendency_parts(levels, rows, lat_two_ways, fold_apart, refs, masked_ref):
-    vertical_ref, mask_ref, stencil_ref, wide_ref, near_ref, lat_ref = refs[:6]
+def inside_kernel(levels, rows, u_ref, t_ref, tv_ref, tw_ref, outer_ref, mask_ref, stencil_ref, out_ref, side_ref, masked_ref):
     stride = rows + 8
+    lane = lax.broadcasted_iota(jnp.int32, (rows, 128), 1)
+    nothing = jnp.zeros((levels, 128), jnp.float32)
+    for k in range(levels):
+        mask = span(mask_ref, k, rows).astype(jnp.float32)
+        west, east = span(stencil_ref, 2 * levels + k, rows), span(stencil_ref, levels + k, rows)
+        side_ref[pl.ds(k * rows, rows), :] = mask * jnp.where(lane == 0, west, jnp.where(lane == 127, east, 0.0))
+    for tracer in range(TRACERS):
+        masked_ref[pl.ds(tracer * levels * stride + 7, levels, stride=stride), :] = nothing
+        masked_ref[pl.ds((tracer * levels + 1) * stride, levels, stride=stride), :] = nothing
+        previous, following = span(outer_ref, tracer, rows), span(outer_ref, TRACERS + tracer, rows)
+        for k in range(levels):
+            j = tracer * levels + k
+            vertical = (
+                span(t_ref, k, rows) * span(u_ref, j, rows)
+                + span(tv_ref, k, rows) * previous
+                + span(tw_ref, k, rows) * following
+            )
+            mask = span(mask_ref, k, rows).astype(jnp.float32)
+            masked = mask * vertical
+            masked_ref[pl.ds(j * stride + 8, rows), :] = masked
+            from_north = masked_ref[pl.ds(j * stride + 9, rows), :]
+            from_south = masked_ref[pl.ds(j * stride + 7, rows), :]
+            from_east = jnp.where(lane == 127, 0.0, pltpu.roll(masked, 127, 1))
+            from_west = jnp.where(lane == 0, 0.0, pltpu.roll(masked, 1, 1))
+            weight = [span(stencil_ref, i * levels + k, rows) for i in range(5)]
+            tendency = (
+                weight[0] * masked
+                + weight[1] * from_east
+                + weight[2] * from_west
+                + weight[3] * from_north
+                + weight[4] * from_south
+            )
+            out_ref[pl.ds(j * rows, rows), :] = vertical + mask * tendency
+
+
+def outside_parts(levels, rows, lat_two_ways, fold_apart, refs, line_ref):
+    inside_ref, side_ref, mask_ref, stencil_ref, wide_ref, near_ref, lat_ref = refs[:7]
     lon_odd = (lax.axis_index("lon") & 1) == 1
     lat_odd = (lax.axis_index("lat") & 1) == 1
     is_top = lax.axis_index("lat") == lax.axis_size("lat") - 1
@@ -248,46 +319,36 @@
     east, west = jnp.where(lon_odd, wide, near), jnp.where(lon_odd, near, wide)
     edges = jnp.where((lane & 1) == 0, pltpu.roll(east, 127, 1), pltpu.roll(west, 1, 1))
     fold_ref, fold_at = (refs[-1], 0) if fold_apart else (wide_ref, rows)
-    for tracer in range(TRACERS):
-        rows_at = pl.ds(tracer * 24, levels)
-        halo = lat_ref[rows_at, :]
-        back = refs[6][rows_at, :] if lat_two_ways else jnp.zeros_like(halo)
+
+    def line(ref, plane, at):
+        return ref[pl.ds(plane * levels * rows + at, levels, stride=rows), :]
+
+    first_mask = line(mask_ref, 0, 0).astype(jnp.float32)
+    last_mask = line(mask_ref, 0, rows - 1).astype(jnp.float32)
+    to_north, to_south = line(stencil_ref, 3, rows - 1), line(stencil_ref, 4, 0)
+    for tracer in range(TRACERS):
+        at = pl.ds(tracer * 24, levels)
+        halo = lat_ref[at, :]
+        back = refs[7][at, :] if lat_two_ways else jnp.zeros_like(halo)
         north, south = jnp.where(lat_odd, back, halo), jnp.where(lat_odd, halo, back)
-        masked_ref[pl.ds(tracer * levels * stride + 7, levels, stride=stride), :] = south
-        masked_ref[pl.ds((tracer * levels + 1) * stride, levels, stride=stride), :] = north
-        for k in range(levels):
-            j = tracer * levels + k
-            masked_ref[pl.ds(j * stride + 8, rows), :] = span(mask_ref, k, rows).astype(jnp.float32) * span(
-                vertical_ref, j, rows
-            )
+        folded = jnp.where(is_top, fold_ref[pl.ds(fold_at + tracer * 24, levels), :], 0.0)
+        line_ref[at, :] = first_mask * (to_south * south)
+        line_ref[pl.ds(48 + tracer * 24, levels), :] = last_mask * (to_north * north + folded)
 
     def next_adjoint(tracer, k):
         j = tracer * levels + k
-        mask = span(mask_ref, k, rows).astype(jnp.float32)
-        masked = masked_ref[pl.ds(j * stride + 8, rows), :]
-        from_north = masked_ref[pl.ds(j * stride + 9, rows), :]
-        from_south = masked_ref[pl.ds(j * stride + 7, rows), :]
-        edge = pltpu.roll(edges, 127 - 2 * j, 1)
-        from_east = jnp.where(lane == 127, edge, pltpu.roll(masked, 127, 1))
-        from_west = jnp.where(lane == 0, edge, pltpu.roll(masked, 1, 1))
-        weight = [span(stencil_ref, i * levels + k, rows) for i in range(5)]
-        tendency = (
-            weight[0] * masked
-            + weight[1] * from_east
-            + weight[2] * from_west
-            + weight[3] * from_north
-            + weight[4] * from_south
-        )
-        folded = fold_ref[pl.ds(fold_at + tracer * 24 + k, 1), :]
-        tendency = tendency + jnp.where((row == rows - 1) & is_top, folded, 0.0)
-        return span(vertical_ref, j, rows) + mask * tendency
+        first = line_ref[pl.ds(tracer * 24 + k, 1), :]
+        last = line_ref[pl.ds(48 + tracer * 24 + k, 1), :]
+        rim = jnp.where(row == 0, first, jnp.where(row == rows - 1, last, 0.0))
+        sides = span(side_ref, k, rows) * pltpu.roll(edges, 127 - 2 * j, 1)
+        return span(inside_ref, j, rows) + sides + rim
 
     return next_adjoint
 
 
 def turn_kernel(levels, rows, lat_two_ways, fold_apart, *refs):
-    *refs, rp_ref, a_ref, c_ref, share_ref, u_ref, b_ref, far_ref, masked_ref = refs
-    read = tendency_parts(levels, rows, lat_two_ways, fold_apart, refs, masked_ref)
+    *refs, rp_ref, a_ref, c_ref, share_ref, u_ref, b_ref, far_ref, line_ref = refs
+    read = outside_parts(levels, rows, lat_two_ways, fold_apart, refs, line_ref)
     local_solve(levels, rows, read, u_ref, b_ref, rp_ref, a_ref, c_ref)
     for tracer in range(TRACERS):
         first, last = span(b_ref, tracer, rows), span(b_ref, TRACERS + tracer, rows)
@@ -295,8 +356,8 @@
 
 
 def last_kernel(levels, rows, lat_two_ways, fold_apart, *refs):
-    *refs, out_ref, masked_ref, held_ref, sems = refs
-    read = tendency_parts(levels, rows, lat_two_ways, fold_apart, refs, masked_ref)
+    *refs, out_ref, line_ref, held_ref, sems = refs
+    read = outside_parts(levels, rows, lat_two_ways, fold_apart, refs, line_ref)
     copies = []
     half = (levels + 1) // 2
     for tracer in range(TRACERS):
@@ -367,13 +428,19 @@
         else:
             more, far = lev_swap(alpha, 3), lev_swap(alpha, 2)
             other = lev_swap(ends, 1)
+        packs, lines = call(
+            functools.partial(edges_kernel, levels, rows),
+            [(3 * rows, width), (6 * 48, width)],
+            (solved, t, tv, tw, mask),
+            [flat],
+        )
         messages = [((rows + (0 if fold_apart else 48)), width), (48, width)]
         messages += [(48, width)] * (lat_two_ways + fold_apart)
-        vertical, lon_message, lat_message, *rest = call(
-            functools.partial(finish_kernel, levels, rows, lat_two_ways, fold_apart, turn_index > 0),
-            [flat] + messages,
-            (ends, other, spikes, other_spikes, far, more, far_beta, solved, t, tv, tw, mask, weights, source),
-            [flat, (48, width)],
+        outer, lon_message, lat_message, *rest = call(
+            functools.partial(send_kernel, levels, rows, lat_two_ways, fold_apart, turn_index > 0),
+            [(2 * TRACERS * rows, width)] + messages,
+            (ends, other, spikes, other_spikes, far, more, far_beta, packs, lines, weights, source),
+            [(48, width)],
         )
         from_lat = lax.ppermute(lat_message, "lat", lat_near)
         from_wide = lax.ppermute(lon_message, "lon", wide_pairs)
@@ -383,21 +450,27 @@
             extra.append(lax.ppermute(rest[0], "lat", lat_wide))
         if fold_apart:
             extra.append(lax.ppermute(rest[-1], "lon", fold_pairs))
-        operands = (vertical, mask, weights, from_wide, from_near, from_lat, *extra)
-        pad = (TRACERS * levels * (rows + 8) + 8, width)
+        inside, sides = call(
+            functools.partial(inside_kernel, levels, rows),
+            [flat, column],
+            (solved, t, tv, tw, outer, mask, weights),
+            [(TRACERS * levels * (rows + 8) + 8, width)],
+        )
+        operands = (inside, sides, mask, weights, from_wide, from_near, from_lat, *extra)
+        lines_held = (96, width)
         if turn_index < STEPS - 1:
             solved, ends, alpha = call(
                 functools.partial(turn_kernel, levels, rows, lat_two_ways, fold_apart),
                 [flat, (4 * rows, width), (2 * rows, width)],
                 (*operands, rp, a, c, share),
-                [pad],
+                [lines_held],
             )
         else:
             out = call(
                 functools.partial(last_kernel, levels, rows, lat_two_ways, fold_apart),
                 [flat],
                 operands,
-                [pad, flat],
+                [lines_held, flat],
                 4,
                 write_in_place=True,
             )[0]

time: 41.5 us -> 40.8 us (0.983)
  waiting for transfers between devices: 18.2 us -> 16.9 us
  Pallas kernels: 3.55 us -> 4.12 us
    ppermute x8, waiting for transfers between devices: 16 us -> 15.4 us  [lev_swap(): lax.ppermute(value, 'lev', [(i, i ^ distance) for i in range(places)])]
    ppermute x2, waiting for transfers between devices: 1.66 us -> 1.07 us  [shards(): from_near = lax.ppermute(lon_message[:rows], 'lon', near_pairs)]
    pallas_call x7 -> x11, Pallas kernels: 3.55 us -> 4.12 us  [call(): pl.pallas_call(kernel, out_shape=[jax.ShapeDtypeStruct(shape, jnp.float32...]
  transfers between devices with their start and end apart: 14 -> 14, of which waited for: 10 -> 10; matrix products, arithmetic and copies ran while one was open for 0% -> 0% of each run, Pallas kernels for 0% -> 3%
where the time goes in v3:
time: 40.8 us; the launch traced here: 40.7 us
  starting transfers between devices  19.4 us (48%)
  waiting for transfers between devices  16.9 us (41%)
  Pallas kernels  4.12 us (10%)
    ppermute x8, waiting for transfers between devices, lev_swap(): lax.ppermute(value, 'lev', [(i, i ^ distance) for i in range(places)])  15.4 us
    ppermute x8, starting transfers between devices, lev_swap(): lax.ppermute(value, 'lev', [(i, i ^ distance) for i in range(places)])  13.6 us
    pallas_call x11, Pallas kernels, call(): pl.pallas_call(kernel, out_shape=[jax.ShapeDtypeStruct(shape, jnp.float32...  4.12 us
    ppermute x2, starting transfers between devices, shards(): from_lat = lax.ppermute(lat_message, 'lat', lat_near)  3.11 us
    ppermute x2, starting transfers between devices, shards(): from_near = lax.ppermute(lon_message[:rows], 'lon', near_pairs)  2.55 us
    ppermute x2, waiting for transfers between devices, shards(): from_near = lax.ppermute(lon_message[:rows], 'lon', near_pairs)  1.07 us
  transfers between devices with their start and end apart: 14, of which 10 were waited for; matrix products, arithmetic and copies ran while one was open for 0% of the time, Pallas kernels for 3%

profile of v3, /device:TPU:0, one launch (start us, length us, event | category | flops | bytes accessed | tf_op | source)
XLA Modules:
  0.0 40.7 jit_solution(12988728985351650880)
XLA Ops:
  0.0 1.2 %shard_map.73 = (f32[37,4,128]{2,1,0:T(4,128)S(1)}, f32[37,4,128]{2,1,0:T(4,128)S(1)}, f32[37,4,128]{2,1,0:T(4,128)S(1)}, f32[37,4,128]{2,1,0:T(4,128)S(1)}, f32[576,128]{1,0:T(8,128)S(1)}) custom-call(f32[72,4,128]{2,1,0:T(4,128)} %thickness_ref.1, f32[72,4,128]{2,1,0:T(4,128)} %diffusivity_ref.1, s32[4,128]{1,0:T(4,128)} %counts_ref.1, f32[576,128]{1,0:T(8,128)} %bitcast.16), custom_call_target="tpu_custom_call" | custom-call | tf_op jit(solution)/shard_map/pallas_call | solution.py:18
  1.2 3.1 %collective-permute-start = (f32[37,4,128]{2,1,0:T(4,128)S(1)}, f32[37,4,128]{2,1,0:T(4,128)S(1)}, u32[]{:S(2)}, u32[]{:S(2)}) collective-permute-start(f32[37,4,128]{2,1,0:T(4,128)S(1)} %get-tuple-element.38), channel_id=1, source_target_pairs={{0,1},{1,0},{2,3},{3,2},{4,5},{5,4},{6,7},{7,6},{8,9},{9,8},{10,11... | collective-permute-start | bytes 227336 | tf_op jit(solution)/shard_map/ppermute | solution.py:388
  4.3 2.6 %collective-permute-start.1 = (f32[37,4,128]{2,1,0:T(4,128)S(1)}, f32[37,4,128]{2,1,0:T(4,128)S(1)}, u32[]{:S(2)}, u32[]{:S(2)}) collective-permute-start(f32[37,4,128]{2,1,0:T(4,128)S(1)} %get-tuple-element.39), channel_id=1, source_target_pairs={{0,2},{1,3},{2,0},{3,1},{4,6},{5,7},{6,4},{7,5},{8,10},{9,11},{10,... | collective-permute-start | bytes 227336 | tf_op jit(solution)/shard_map/ppermute | solution.py:388
  6.9 0.0 collective-permute-start.2
  6.9 0.0 copy-start.2
  6.9 0.0 collective-permute-done.refs_1_
  6.9 5.3 %collective-permute-done.1.refs_2_ = f32[37,4,128]{2,1,0:T(4,128)S(1)} collective-permute-done((f32[37,4,128]{2,1,0:T(4,128)S(1)}, f32[37,4,128]{2,1,0:T(4,128)S(1)}, u32[]{:S(2)}, u32[]{:S(2)}) %collective-permute-start.1) | collective-permute-done | bytes 75808 | tf_op jit(solution)/shard_map/ppermute | solution.py:388
  12.2 0.9 %collective-permute-done.2.refs_3_ = f32[37,4,128]{2,1,0:T(4,128)S(1)} collective-permute-done((f32[37,4,128]{2,1,0:T(4,128)S(1)}, f32[37,4,128]{2,1,0:T(4,128)S(1)}, u32[]{:S(2)}, u32[]{:S(2)}) %collective-permute-start.2) | collective-permute-done | bytes 75808 | tf_op jit(solution)/shard_map/ppermute | solution.py:388
  13.2 0.0 copy-start.1
  13.2 0.0 copy-start
  13.2 0.2 shard_map.74
  13.4 1.3 %collective-permute-start.3 = (f32[128,128]{1,0:T(8,128)S(1)}, f32[128,128]{1,0:T(8,128)S(1)}, u32[]{:S(2)}, u32[]{:S(2)}) collective-permute-start(f32[128,128]{1,0:T(8,128)S(1)} %get-tuple-element.46.mine_ref.refs_0_.refs_2_), channel_id=1, source_target_pairs={{0,1},{1,0},{2,3},{3,2},{4,5},{5,4},{6,7},{7,6},{8,9},{9,8},{10,11... | collective-permute-start | bytes 196616 | tf_op jit(solution)/shard_map/ppermute | solution.py:388
  14.7 0.0 copy-done.2
  14.7 3.0 %collective-permute-done.3.other_ref.refs_1_.refs_3_ = f32[128,128]{1,0:T(8,128)S(1)} collective-permute-done((f32[128,128]{1,0:T(8,128)S(1)}, f32[128,128]{1,0:T(8,128)S(1)}, u32[]{:S(2)}, u32[]{:S(2)}) %collective-permute-start.3) | collective-permute-done | bytes 65568 | tf_op jit(solution)/shard_map/ppermute | solution.py:388
  17.8 2.6 %collective-permute-start.4 = (f32[48,128]{1,0:T(8,128)S(1)}, f32[48,128]{1,0:T(8,128)S(1)}, u32[]{:S(2)}, u32[]{:S(2)}) collective-permute-start(f32[48,128]{1,0:T(8,128)S(1)} %get-tuple-element.47), channel_id=1, source_target_pairs={{0,2},{1,3},{2,0},{3,1},{4,6},{5,7},{6,4},{7,5},{8,10},{9,11},{10,... | collective-permute-start | bytes 73736 | tf_op jit(solution)/shard_map/ppermute | solution.py:388
  20.4 0.1 select_reduce_fusion
  20.5 0.0 copy-done.1
  20.5 0.3 shard_map.76
  20.8 1.8 %collective-permute-done.4.refs_4_.refs_5_.refs_6_ = f32[48,128]{1,0:T(8,128)S(1)} collective-permute-done((f32[48,128]{1,0:T(8,128)S(1)}, f32[48,128]{1,0:T(8,128)S(1)}, u32[]{:S(2)}, u32[]{:S(2)}) %collective-permute-start.4) | collective-permute-done | bytes 24608 | tf_op jit(solution)/shard_map/ppermute | solution.py:388
  22.6 0.0 copy-done
  22.6 0.1 shard_map.77
  22.7 0.1 collective-permute-start.5
  22.8 1.6 %collective-permute-start.7 = (f32[48,128]{1,0:T(8,128)S(1)}, f32[48,128]{1,0:T(8,128)S(1)}, u32[]{:S(2)}, u32[]{:S(2)}) collective-permute-start(f32[48,128]{1,0:T(8,128)S(1)} %get-tuple-element.54), channel_id=1, source_target_pairs={{0,16},{16,0},{1,17},{17,1},{2,18},{18,2},{3,19},{19,3},{4,20},{20... | collective-permute-start | bytes 73736 | tf_op jit(solution)/shard_map/ppermute | solution.py:445
  24.4 1.3 %collective-permute-start.6 = (f32[16,128]{1,0:T(8,128)S(1)}, f32[16,128]{1,0:T(8,128)S(1)}, u32[]{:S(2)}, u32[]{:S(2)}) collective-permute-start(f32[16,128]{1,0:T(8,128)S(1)} %slice.6), channel_id=1, source_target_pairs={{0,4},{4,0},{8,12},{12,8},{1,5},{5,1},{9,13},{13,9},{2,6},{6,2},{1... | collective-permute-start | bytes 24584 | tf_op jit(solution)/shard_map/ppermute | solution.py:447
  25.6 0.3 shard_map.78
  25.9 0.5 %collective-permute-done.6.refs_5_ = f32[16,128]{1,0:T(8,128)S(1)} collective-permute-done((f32[16,128]{1,0:T(8,128)S(1)}, f32[16,128]{1,0:T(8,128)S(1)}, u32[]{:S(2)}, u32[]{:S(2)}) %collective-permute-start.6) | collective-permute-done | bytes 8224 | tf_op jit(solution)/shard_map/ppermute | solution.py:447
  26.5 0.2 collective-permute-done.7.refs_6_
  26.7 0.0 collective-permute-done.5.refs_4_
  26.7 0.3 shard_map.79
  27.0 1.3 %collective-permute-start.8 = (f32[64,128]{1,0:T(8,128)S(1)}, f32[64,128]{1,0:T(8,128)S(1)}, u32[]{:S(2)}, u32[]{:S(2)}) collective-permute-start(f32[64,128]{1,0:T(8,128)S(1)} %get-tuple-element.60.refs_0_), channel_id=1, source_target_pairs={{0,1},{1,0},{2,3},{3,2},{4,5},{5,4},{6,7},{7,6},{8,9},{9,8},{10,11... | collective-permute-start | bytes 98312 | tf_op jit(solution)/shard_map/ppermute | solution.py:388
  28.3 2.7 %collective-permute-start.10 = (f32[32,128]{1,0:T(8,128)S(1)}, f32[32,128]{1,0:T(8,128)S(1)}, u32[]{:S(2)}, u32[]{:S(2)}) collective-permute-start(f32[32,128]{1,0:T(8,128)S(1)} %get-tuple-element.61), channel_id=1, source_target_pairs={{0,3},{1,2},{2,1},{3,0},{4,7},{5,6},{6,5},{7,4},{8,11},{9,10},{10,... | collective-permute-start | bytes 49160 | tf_op jit(solution)/shard_map/ppermute | solution.py:388
  31.0 0.0 collective-permute-start.9
  31.0 0.3 shard_map.80
  31.3 2.5 %collective-permute-done.10.refs_5_ = f32[32,128]{1,0:T(8,128)S(1)} collective-permute-done((f32[32,128]{1,0:T(8,128)S(1)}, f32[32,128]{1,0:T(8,128)S(1)}, u32[]{:S(2)}, u32[]{:S(2)}) %collective-permute-start.10) | collective-permute-done | bytes 16416 | tf_op jit(solution)/shard_map/ppermute | solution.py:388
  33.8 1.8 %collective-permute-done.9.refs_4_ = f32[32,128]{1,0:T(8,128)S(1)} collective-permute-done((f32[32,128]{1,0:T(8,128)S(1)}, f32[32,128]{1,0:T(8,128)S(1)}, u32[]{:S(2)}, u32[]{:S(2)}) %collective-permute-start.9) | collective-permute-done | bytes 16416 | tf_op jit(solution)/shard_map/ppermute | solution.py:388
  35.6 0.0 collective-permute-done.8.refs_1_
  35.7 0.1 shard_map.81
  35.8 0.1 collective-permute-start.11
  35.9 1.6 %collective-permute-start.13 = (f32[48,128]{1,0:T(8,128)S(1)}, f32[48,128]{1,0:T(8,128)S(1)}, u32[]{:S(2)}, u32[]{:S(2)}) collective-permute-start(f32[48,128]{1,0:T(8,128)S(1)} %get-tuple-element.68), channel_id=1, source_target_pairs={{0,16},{16,0},{1,17},{17,1},{2,18},{18,2},{3,19},{19,3},{4,20},{20... | collective-permute-start | bytes 73736 | tf_op jit(solution)/shard_map/ppermute | solution.py:445
  37.4 1.3 %collective-permute-start.12 = (f32[16,128]{1,0:T(8,128)S(1)}, f32[16,128]{1,0:T(8,128)S(1)}, u32[]{:S(2)}, u32[]{:S(2)}) collective-permute-start(f32[16,128]{1,0:T(8,128)S(1)} %slice.7), channel_id=1, source_target_pairs={{0,4},{4,0},{8,12},{12,8},{1,5},{5,1},{9,13},{13,9},{2,6},{6,2},{1... | collective-permute-start | bytes 24584 | tf_op jit(solution)/shard_map/ppermute | solution.py:447
  38.7 0.3 shard_map.82
  39.0 0.5 %collective-permute-done.12.refs_5_ = f32[16,128]{1,0:T(8,128)S(1)} collective-permute-done((f32[16,128]{1,0:T(8,128)S(1)}, f32[16,128]{1,0:T(8,128)S(1)}, u32[]{:S(2)}, u32[]{:S(2)}) %collective-permute-start.12) | collective-permute-done | bytes 8224 | tf_op jit(solution)/shard_map/ppermute | solution.py:447
  39.5 0.2 collective-permute-done.13.refs_6_
  39.8 0.0 collective-permute-done.11.refs_4_
  39.8 0.9 %shard_map.83 = f32[576,128]{1,0:T(8,128)} custom-call(f32[576,128]{1,0:T(8,128)S(1)} %get-tuple-element.65.refs_0_, f32[288,128]{1,0:T(8,128)S(1)} %get-tuple-element.66.refs_1_, s32[288,128]{1,0:T(8,128)S(1)} %bitcast.15, f32[1440,128]{1,0:T(8,128)S(1)} %bitcast.9, f32[64,128]{1,0:T(8,128)S(1)} %collective-permute-done.11.refs_4_, ...), custom_call_target="tpu_custom_call" | custom-call | tf_op jit(solution)/shard_map/pallas_call | solution.py:18
  (5 shorter events, 0.0 us)
Async XLA Ops:
  1.2 5.7 %collective-permute-start = (f32[37,4,128]{2,1,0:T(4,128)S(1)}, f32[37,4,128]{2,1,0:T(4,128)S(1)}, u32[]{:S(2)}, u32[]{:S(2)}) collective-permute-start(f32[37,4,128]{2,1,0:T(4,128)S(1)} %get-tuple-element.38), channel_id=1, source_target_pairs={{0,1},{1,0},{2,3},{3,2},{4,5},{5,4},{6,7},{7,6},{8,9},{9,8},{10,11... | collective-permute-start | bytes 227336 | tf_op jit(solution)/shard_map/ppermute | solution.py:388
  4.3 7.9 %collective-permute-start.1 = (f32[37,4,128]{2,1,0:T(4,128)S(1)}, f32[37,4,128]{2,1,0:T(4,128)S(1)}, u32[]{:S(2)}, u32[]{:S(2)}) collective-permute-start(f32[37,4,128]{2,1,0:T(4,128)S(1)} %get-tuple-element.39), channel_id=1, source_target_pairs={{0,2},{1,3},{2,0},{3,1},{4,6},{5,7},{6,4},{7,5},{8,10},{9,11},{10,... | collective-permute-start | bytes 227336 | tf_op jit(solution)/shard_map/ppermute | solution.py:388
  6.9 6.3 %collective-permute-start.2 = (f32[37,4,128]{2,1,0:T(4,128)S(1)}, f32[37,4,128]{2,1,0:T(4,128)S(1)}, u32[]{:S(2)}, u32[]{:S(2)}) collective-permute-start(f32[37,4,128]{2,1,0:T(4,128)S(1)} %get-tuple-element.40), channel_id=1, source_target_pairs={{0,3},{1,2},{2,1},{3,0},{4,7},{5,6},{6,5},{7,4},{8,11},{9,10},{10,... | collective-permute-start | bytes 227336 | tf_op jit(solution)/shard_map/ppermute | solution.py:388
  6.9 7.8 %copy-start.2 = (s32[128]{0:T(128)S(1)}, s32[128]{0:T(128)}, u32[]{:S(2)}) copy-start(s32[128]{0:T(128)} %param.13) | copy-start | bytes 1540
  13.2 7.3 %copy-start.1 = (s32[18,16,128]{2,1,0:T(8,128)S(1)}, s32[18,16,128]{2,1,0:T(8,128)}, u32[]{:S(2)}) copy-start(s32[18,16,128]{2,1,0:T(8,128)} %param.9) | copy-start | bytes 442372
  13.2 9.4 %copy-start = (f32[5,18,16,128]{3,2,1,0:T(8,128)S(1)}, f32[5,18,16,128]{3,2,1,0:T(8,128)}, u32[]{:S(2)}) copy-start(f32[5,18,16,128]{3,2,1,0:T(8,128)} %param.8) | copy-start | bytes 2211844
  13.4 4.3 %collective-permute-start.3 = (f32[128,128]{1,0:T(8,128)S(1)}, f32[128,128]{1,0:T(8,128)S(1)}, u32[]{:S(2)}, u32[]{:S(2)}) collective-permute-start(f32[128,128]{1,0:T(8,128)S(1)} %get-tuple-element.46.mine_ref.refs_0_.refs_2_), channel_id=1, source_target_pairs={{0,1},{1,0},{2,3},{3,2},{4,5},{5,4},{6,7},{7,6},{8,9},{9,8},{10,11... | collective-permute-start | bytes 196616 | tf_op jit(solution)/shard_map/ppermute | solution.py:388
  17.8 4.8 %collective-permute-start.4 = (f32[48,128]{1,0:T(8,128)S(1)}, f32[48,128]{1,0:T(8,128)S(1)}, u32[]{:S(2)}, u32[]{:S(2)}) collective-permute-start(f32[48,128]{1,0:T(8,128)S(1)} %get-tuple-element.47), channel_id=1, source_target_pairs={{0,2},{1,3},{2,0},{3,1},{4,6},{5,7},{6,4},{7,5},{8,10},{9,11},{10,... | collective-permute-start | bytes 73736 | tf_op jit(solution)/shard_map/ppermute | solution.py:388
  22.7 4.0 %collective-permute-start.5 = (f32[64,128]{1,0:T(8,128)S(1)}, f32[64,128]{1,0:T(8,128)S(1)}, u32[]{:S(2)}, u32[]{:S(2)}) collective-permute-start(f32[64,128]{1,0:T(8,128)S(1)} %get-tuple-element.53), channel_id=1, source_target_pairs={{0,12},{4,8},{8,4},{12,0},{1,13},{5,9},{9,5},{13,1},{2,14},{6,10},... | collective-permute-start | bytes 98312 | tf_op jit(solution)/shard_map/ppermute | solution.py:446
  22.8 3.9 %collective-permute-start.7 = (f32[48,128]{1,0:T(8,128)S(1)}, f32[48,128]{1,0:T(8,128)S(1)}, u32[]{:S(2)}, u32[]{:S(2)}) collective-permute-start(f32[48,128]{1,0:T(8,128)S(1)} %get-tuple-element.54), channel_id=1, source_target_pairs={{0,16},{16,0},{1,17},{17,1},{2,18},{18,2},{3,19},{19,3},{4,20},{20... | collective-permute-start | bytes 73736 | tf_op jit(solution)/shard_map/ppermute | solution.py:445
  24.4 2.1 %collective-permute-start.6 = (f32[16,128]{1,0:T(8,128)S(1)}, f32[16,128]{1,0:T(8,128)S(1)}, u32[]{:S(2)}, u32[]{:S(2)}) collective-permute-start(f32[16,128]{1,0:T(8,128)S(1)} %slice.6), channel_id=1, source_target_pairs={{0,4},{4,0},{8,12},{12,8},{1,5},{5,1},{9,13},{13,9},{2,6},{6,2},{1... | collective-permute-start | bytes 24584 | tf_op jit(solution)/shard_map/ppermute | solution.py:447
  27.0 8.7 %collective-permute-start.8 = (f32[64,128]{1,0:T(8,128)S(1)}, f32[64,128]{1,0:T(8,128)S(1)}, u32[]{:S(2)}, u32[]{:S(2)}) collective-permute-start(f32[64,128]{1,0:T(8,128)S(1)} %get-tuple-element.60.refs_0_), channel_id=1, source_target_pairs={{0,1},{1,0},{2,3},{3,2},{4,5},{5,4},{6,7},{7,6},{8,9},{9,8},{10,11... | collective-permute-start | bytes 98312 | tf_op jit(solution)/shard_map/ppermute | solution.py:388
  28.3 5.5 %collective-permute-start.10 = (f32[32,128]{1,0:T(8,128)S(1)}, f32[32,128]{1,0:T(8,128)S(1)}, u32[]{:S(2)}, u32[]{:S(2)}) collective-permute-start(f32[32,128]{1,0:T(8,128)S(1)} %get-tuple-element.61), channel_id=1, source_target_pairs={{0,3},{1,2},{2,1},{3,0},{4,7},{5,6},{6,5},{7,4},{8,11},{9,10},{10,... | collective-permute-start | bytes 49160 | tf_op jit(solution)/shard_map/ppermute | solution.py:388
  31.0 4.6 %collective-permute-start.9 = (f32[32,128]{1,0:T(8,128)S(1)}, f32[32,128]{1,0:T(8,128)S(1)}, u32[]{:S(2)}, u32[]{:S(2)}) collective-permute-start(f32[32,128]{1,0:T(8,128)S(1)} %get-tuple-element.61), channel_id=1, source_target_pairs={{0,2},{1,3},{2,0},{3,1},{4,6},{5,7},{6,4},{7,5},{8,10},{9,11},{10,... | collective-permute-start | bytes 49160 | tf_op jit(solution)/shard_map/ppermute | solution.py:388
  35.8 4.0 %collective-permute-start.11 = (f32[64,128]{1,0:T(8,128)S(1)}, f32[64,128]{1,0:T(8,128)S(1)}, u32[]{:S(2)}, u32[]{:S(2)}) collective-permute-start(f32[64,128]{1,0:T(8,128)S(1)} %get-tuple-element.67), channel_id=1, source_target_pairs={{0,12},{4,8},{8,4},{12,0},{1,13},{5,9},{9,5},{13,1},{2,14},{6,10},... | collective-permute-start | bytes 98312 | tf_op jit(solution)/shard_map/ppermute | solution.py:446
  35.9 3.9 %collective-permute-start.13 = (f32[48,128]{1,0:T(8,128)S(1)}, f32[48,128]{1,0:T(8,128)S(1)}, u32[]{:S(2)}, u32[]{:S(2)}) collective-permute-start(f32[48,128]{1,0:T(8,128)S(1)} %get-tuple-element.68), channel_id=1, source_target_pairs={{0,16},{16,0},{1,17},{17,1},{2,18},{18,2},{3,19},{19,3},{4,20},{20... | collective-permute-start | bytes 73736 | tf_op jit(solution)/shard_map/ppermute | solution.py:445
  37.4 2.1 %collective-permute-start.12 = (f32[16,128]{1,0:T(8,128)S(1)}, f32[16,128]{1,0:T(8,128)S(1)}, u32[]{:S(2)}, u32[]{:S(2)}) collective-permute-start(f32[16,128]{1,0:T(8,128)S(1)} %slice.7), channel_id=1, source_target_pairs={{0,4},{4,0},{8,12},{12,8},{1,5},{5,1},{9,13},{13,9},{2,6},{6,2},{1... | collective-permute-start | bytes 24584 | tf_op jit(solution)/shard_map/ppermute | solution.py:447

commit v4 on v3

--- a/solution.py
+++ b/solution.py
@@ -28,6 +28,23 @@
 
 def span(ref, index, rows):
     return ref[pl.ds(index * rows, rows), :]
+
+
+def end_values(part, levels):
+    t = [part[k] for k in range(levels)]
+    i = [part[levels + k] for k in range(levels + 1)]
+    high, low = t[0] + i[0], jnp.ones_like(t[0])
+    back_high, back_low = t[-1] + i[-1], jnp.ones_like(t[0])
+    through = jnp.ones_like(t[0])
+    for k in range(1, levels):
+        ahead = high + i[k] * low
+        high, low = t[k] * ahead + i[k] * high, ahead
+        j = levels - k
+        behind = back_high + i[j] * back_low
+        back_high, back_low = t[j - 1] * behind + i[j] * back_high, behind
+        through = through * i[k]
+    scale = 1.0 / (high + i[-1] * low)
+    return i[0] * back_low * scale, i[0] * through * scale, through * i[-1] * scale, i[-1] * low * scale
 
 
 def pack_kernel(levels, places, thickness_ref, diffusivity_ref, counts_ref, adj_ref, *refs):
@@ -53,8 +70,21 @@
             level = jnp.full(counts.shape, start + k, jnp.int32)
             wet = (level >= 1) & (level < counts)
             out_refs[distance][levels + k] = jnp.where(wet, held_ref[jnp.minimum(start + k, last)], 0.0)
-    for copy in ahead[2:]:
+    for copy in ahead[2:-1]:
         copy.wait()
+    spikes = [end_values(out_refs[distance], levels) for distance in range(places)]
+    odd = (me & 1) == 1
+    base = 2 * TRACERS
+    none = [None] * base
+    for pair in range(2):
+        one, two = spikes[2 * pair], spikes[2 * pair + 1]
+        p = none + [jnp.where(odd, y, x) for x, y in zip(one, two)]
+        q = none + [jnp.where(odd, x, y) for x, y in zip(one, two)]
+        beta = pair_spikes(p, q, (me < 2) == (pair == 0))[-1]
+        for distance in (2 - 2 * pair, 3 - 2 * pair):
+            for n, value in enumerate((*spikes[distance ^ 1], beta)):
+                out_refs[distance][2 * levels + 1 + n] = value
+    ahead[-1].wait()
 
 
 def local_solve(levels, rows, read, u_ref, b_ref, rp_ref, a_ref, c_ref):
@@ -75,7 +105,7 @@
 
 def first_kernel(levels, places, strip, *refs):
     parts, refs = refs[:places], refs[places:]
-    adj_ref, u_ref, b_ref, rp_ref, a_ref, c_ref, t_ref, tv_ref, tw_ref, i_ref = refs
+    adj_ref, u_ref, b_ref, alpha_ref, share_ref, static_ref, rp_ref, a_ref, c_ref, t_ref, tv_ref, tw_ref, i_ref = refs
     rows = strip * places
     me = lax.axis_index("lev")
     for place in range(places):
@@ -89,6 +119,8 @@
                     t_ref[pl.ds(k * rows + offset, strip), :] = part[k]
                 for k in range(levels + 1):
                     i_ref[pl.ds(k * rows + offset, strip), :] = part[levels + k]
+                for n in range(5):
+                    static_ref[pl.ds((4 + n) * rows + offset, strip), :] = part[2 * levels + 1 + n]
 
     inner = span(i_ref, 0, rows)
     high = span(t_ref, 0, rows) + inner
@@ -110,9 +142,8 @@
             low = ahead
             inner = outer
     w = span(c_ref, levels - 1, rows)
-    base = 2 * TRACERS
-    b_ref[pl.ds((base + 1) * rows, rows), :] = v
-    b_ref[pl.ds((base + 3) * rows, rows), :] = w
+    static_ref[pl.ds(1 * rows, rows), :] = v
+    static_ref[pl.ds(3 * rows, rows), :] = w
     for k in range(levels - 1, -1, -1):
         at = pl.ds(k * rows, rows)
         if k < levels - 1:
@@ -122,19 +153,35 @@
         t = span(t_ref, k, rows)
         tv_ref[at, :] = t * v
         tw_ref[at, :] = t * w
-    b_ref[pl.ds(base * rows, rows), :] = v
-    b_ref[pl.ds((base + 2) * rows, rows), :] = w
+    static_ref[pl.ds(0 * rows, rows), :] = v
+    static_ref[pl.ds(2 * rows, rows), :] = w
+    odd = (me & 1) == 1
+    p, q = pair_values(rows, odd, None, None, static_ref)
+    _, share_p, share_q, _ = pair_spikes(p, q, me < 2)
+    for i in range(2):
+        share_ref[pl.ds(i * rows, rows), :] = jnp.where(odd, share_q[i], share_p[i])
     local_solve(
         levels, rows, lambda tracer, k: span(adj_ref, tracer * levels + k, rows), u_ref, b_ref, rp_ref, a_ref, c_ref
     )
-
-
-def pair_values(rows, odd, mine_ref, other_ref, spikes_ref, other_spikes_ref):
+    own_share(rows, b_ref, share_ref, alpha_ref)
+
+
+def own_share(rows, b_ref, share_ref, alpha_ref):
+    for tracer in range(TRACERS):
+        first, last = span(b_ref, tracer, rows), span(b_ref, TRACERS + tracer, rows)
+        alpha_ref[pl.ds(tracer * rows, rows), :] = span(share_ref, 0, rows) * first + span(share_ref, 1, rows) * last
+
+
+def pair_values(rows, odd, mine_ref, other_ref, static_ref):
     base = 2 * TRACERS
-    mine = [span(mine_ref, i, rows) for i in range(base)] + [span(spikes_ref, base + i, rows) for i in range(4)]
-    other = [span(other_ref, i, rows) for i in range(base)] + [span(other_spikes_ref, base + i, rows) for i in range(4)]
-    upper = [jnp.where(odd, o, m) for m, o in zip(mine, other)]
-    lower = [jnp.where(odd, m, o) for m, o in zip(mine, other)]
+    mine, other = [], []
+    for i in range(base):
+        mine.append(span(mine_ref, i, rows) if mine_ref is not None else None)
+        other.append(span(other_ref, i, rows) if other_ref is not None else None)
+    mine += [span(static_ref, i, rows) for i in range(4)]
+    other += [span(static_ref, 4 + i, rows) for i in range(4)]
+    upper = [None if m is None else jnp.where(odd, o, m) for m, o in zip(mine, other)]
+    lower = [None if m is None else jnp.where(odd, m, o) for m, o in zip(mine, other)]
     return upper, lower
 
 
@@ -158,18 +205,6 @@
         + share_q[0] * q[tracer]
         + share_q[1] * q[TRACERS + tracer]
     )
-
-
-def merge_kernel(rows, mine_ref, other_ref, out_ref, share_ref):
-    me = lax.axis_index("lev")
-    odd = (me & 1) == 1
-    p, q = pair_values(rows, odd, mine_ref, other_ref, mine_ref, other_ref)
-    _, share_p, share_q, beta = pair_spikes(p, q, me < 2)
-    for tracer in range(TRACERS):
-        out_ref[pl.ds(tracer * rows, rows), :] = pair_alpha(p, q, share_p, share_q, tracer)
-    out_ref[pl.ds(TRACERS * rows, rows), :] = beta
-    for i in range(2):
-        share_ref[pl.ds(i * rows, rows), :] = jnp.where(odd, share_q[i], share_p[i])
 
 
 def edges_kernel(levels, rows, u_ref, t_ref, tv_ref, tw_ref, mask_ref, pack_ref, line_ref, held_ref):
@@ -198,22 +233,19 @@
                 ]
 
 
-def send_kernel(levels, rows, lat_two_ways, fold_apart, two_shares, *refs):
-    (
-        mine_ref, other_ref, spikes_ref, other_spikes_ref, far_ref, more_ref, far_beta_ref,
-        pack_ref, line_ref, stencil_ref, source_ref,
-    ) = refs[:11]
-    out_refs, fold_ref = refs[11:-1], refs[-1]
+def send_kernel(levels, rows, lat_two_ways, fold_apart, *refs):
+    mine_ref, other_ref, far_ref, more_ref, static_ref, pack_ref, line_ref, stencil_ref, source_ref = refs[:9]
+    out_refs, fold_ref = refs[9:-1], refs[-1]
     outer_ref, lon_ref, lat_ref = out_refs[:3]
     me = lax.axis_index("lev")
     odd = (me & 1) == 1
     is_upper = me < 2
-    p, q = pair_values(rows, odd, mine_ref, other_ref, spikes_ref, other_spikes_ref)
+    p, q = pair_values(rows, odd, mine_ref, other_ref, static_ref)
     base = 2 * TRACERS
     vl_p, wl_p = p[base + 1], p[base + 3]
     vf_q, wf_q = q[base], q[base + 2]
     det, share_p, share_q, beta = pair_spikes(p, q, is_upper)
-    far_beta = span(far_beta_ref, TRACERS, rows)
+    far_beta = span(static_ref, 8, rows)
     far_det = 1.0 / (1.0 - beta * far_beta)
     zero = jnp.zeros_like(det)
     lane = lax.broadcasted_iota(jnp.int32, (rows, 128), 1)
@@ -222,9 +254,7 @@
     fold_ref[...] = jnp.zeros_like(fold_ref)
     sides = []
     for tracer in range(TRACERS):
-        far = span(far_ref, tracer, rows)
-        if two_shares:
-            far = far + span(more_ref, tracer, rows)
+        far = span(far_ref, tracer, rows) + span(more_ref, tracer, rows)
         outside = (far + far_beta * pair_alpha(p, q, share_p, share_q, tracer)) * far_det
         above = jnp.where(is_upper, zero, outside)
         below = jnp.where(is_upper, outside, zero)
@@ -350,9 +380,7 @@
     *refs, rp_ref, a_ref, c_ref, share_ref, u_ref, b_ref, far_ref, line_ref = refs
     read = outside_parts(levels, rows, lat_two_ways, fold_apart, refs, line_ref)
     local_solve(levels, rows, read, u_ref, b_ref, rp_ref, a_ref, c_ref)
-    for tracer in range(TRACERS):
-        first, last = span(b_ref, tracer, rows), span(b_ref, TRACERS + tracer, rows)
-        far_ref[pl.ds(tracer * rows, rows), :] = span(share_ref, 0, rows) * first + span(share_ref, 1, rows) * last
+    own_share(rows, b_ref, share_ref, far_ref)
 
 
 def last_kernel(levels, rows, lat_two_ways, fold_apart, *refs):
@@ -397,7 +425,7 @@
 
     own, *parts, near_adj = call(
         functools.partial(pack_kernel, levels, places),
-        [(2 * levels + 1, strip, width)] * places + [flat],
+        [(2 * levels + 6, strip, width)] * places + [flat],
         (thickness, diffusivity, level_counts, adj),
         [thickness.shape, (level_counts.shape, jnp.int32)],
         3 + places,
@@ -411,23 +439,15 @@
     hit = targets[:, None] == lax.broadcasted_iota(jnp.int32, (width, width), 1)
     source = jnp.broadcast_to(jnp.sum(jnp.where(hit, here, 0), axis=0)[None], (8, width))
 
-    solved, ends, rp, a, c, t, tv, tw = call(
+    solved, ends, alpha, share, static, rp, a, c, t, tv, tw = call(
         functools.partial(first_kernel, levels, places, strip),
-        [flat, (8 * rows, width)] + [column] * 6,
+        [flat, (4 * rows, width), (2 * rows, width), (2 * rows, width), (9 * rows, width)] + [column] * 6,
         (*parts, near_adj),
         [((levels + 1) * rows, width)],
     )
     for turn_index in range(STEPS):
-        if turn_index == 0:
-            other = lev_swap(ends, 1)
-            near, share = call(
-                functools.partial(merge_kernel, rows), [((TRACERS + 1) * rows, width), (2 * rows, width)], (ends, other)
-            )
-            far = more = far_beta = lev_swap(near, 2)
-            spikes, other_spikes = ends, other
-        else:
-            more, far = lev_swap(alpha, 3), lev_swap(alpha, 2)
-            other = lev_swap(ends, 1)
+        more, far = lev_swap(alpha, 3), lev_swap(alpha, 2)
+        other = lev_swap(ends, 1)
         packs, lines = call(
             functools.partial(edges_kernel, levels, rows),
             [(3 * rows, width), (6 * 48, width)],
@@ -437,9 +457,9 @@
         messages = [((rows + (0 if fold_apart else 48)), width), (48, width)]
         messages += [(48, width)] * (lat_two_ways + fold_apart)
         outer, lon_message, lat_message, *rest = call(
-            functools.partial(send_kernel, levels, rows, lat_two_ways, fold_apart, turn_index > 0),
+            functools.partial(send_kernel, levels, rows, lat_two_ways, fold_apart),
             [(2 * TRACERS * rows, width)] + messages,
-            (ends, other, spikes, other_spikes, far, more, far_beta, packs, lines, weights, source),
+            (ends, other, far, more, static, packs, lines, weights, source),
             [(48, width)],
         )
         from_lat = lax.ppermute(lat_message, "lat", lat_near)

time: 40.8 us -> 40.2 us (0.985)
  waiting for transfers between devices: 16.9 us -> 15.1 us
  local copies, waits for them, and re-layouts: 0.02 us -> 0.67 us
  starting transfers between devices: 19.4 us -> 19.9 us
    ppermute x8 -> x9, waiting for transfers between devices: 15.4 us -> 13.6 us  [lev_swap(): lax.ppermute(value, 'lev', [(i, i ^ distance) for i in range(places)])]
    unnamed x6, local copies, waits for them, and re-layouts: 0.01 us -> 0.66 us
    ppermute x8 -> x9, starting transfers between devices: 13.6 us -> 14.1 us  [lev_swap(): lax.ppermute(value, 'lev', [(i, i ^ distance) for i in range(places)])]
    pallas_call x11 -> x10, Pallas kernels: 4.12 us -> 4.18 us  [call(): pl.pallas_call(kernel, out_shape=[jax.ShapeDtypeStruct(shape, jnp.float32...]
  transfers between devices with their start and end apart: 14 -> 15, of which waited for: 10 -> 8; matrix products, arithmetic and copies ran while one was open for 0% -> 0% of each run, Pallas kernels for 3% -> 3%
where the time goes in v4:
time: 40.2 us; the launch traced here: 40 us
  starting transfers between devices  19.9 us (50%)
  waiting for transfers between devices  15.1 us (38%)
  Pallas kernels  4.18 us (10%)
  local copies, waits for them, and re-layouts  0.67 us (2%)
    ppermute x9, starting transfers between devices, lev_swap(): lax.ppermute(value, 'lev', [(i, i ^ distance) for i in range(places)])  14.1 us
    ppermute x9, waiting for transfers between devices, lev_swap(): lax.ppermute(value, 'lev', [(i, i ^ distance) for i in range(places)])  13.6 us
    pallas_call x10, Pallas kernels, call(): pl.pallas_call(kernel, out_shape=[jax.ShapeDtypeStruct(shape, jnp.float32...  4.18 us
    ppermute x2, starting transfers between devices, shards(): from_lat = lax.ppermute(lat_message, 'lat', lat_near)  3.11 us
    ppermute x2, starting transfers between devices, shards(): from_near = lax.ppermute(lon_message[:rows], 'lon', near_pairs)  2.55 us
    ppermute x2, waiting for transfers between devices, shards(): from_near = lax.ppermute(lon_message[:rows], 'lon', near_pairs)  1.08 us
  transfers between devices with their start and end apart: 15, of which 8 were waited for; matrix products, arithmetic and copies ran while one was open for 0% of the time, Pallas kernels for 3%

profile of v4, /device:TPU:0, one launch (start us, length us, event | category | flops | bytes accessed | tf_op | source)
XLA Modules:
  0.0 40.0 jit_solution(2512802196860198219)
XLA Ops:
  0.0 1.2 %shard_map.73 = (f32[42,4,128]{2,1,0:T(4,128)S(1)}, f32[42,4,128]{2,1,0:T(4,128)S(1)}, f32[42,4,128]{2,1,0:T(4,128)S(1)}, f32[42,4,128]{2,1,0:T(4,128)S(1)}, f32[576,128]{1,0:T(8,128)S(1)}) custom-call(f32[72,4,128]{2,1,0:T(4,128)} %thickness_ref.1, f32[72,4,128]{2,1,0:T(4,128)} %diffusivity_ref.1, s32[4,128]{1,0:T(4,128)} %counts_ref.1, f32[576,128]{1,0:T(8,128)} %bitcast.16), custom_call_target="tpu_custom_call" | custom-call | tf_op jit(solution)/shard_map/pallas_call | solution.py:18
  1.2 3.1 %collective-permute-start = (f32[42,4,128]{2,1,0:T(4,128)S(1)}, f32[42,4,128]{2,1,0:T(4,128)S(1)}, u32[]{:S(2)}, u32[]{:S(2)}) collective-permute-start(f32[42,4,128]{2,1,0:T(4,128)S(1)} %get-tuple-element.39), channel_id=1, source_target_pairs={{0,1},{1,0},{2,3},{3,2},{4,5},{5,4},{6,7},{7,6},{8,9},{9,8},{10,11... | collective-permute-start | bytes 258056 | tf_op jit(solution)/shard_map/ppermute | solution.py:416
  4.4 2.6 %collective-permute-start.1 = (f32[42,4,128]{2,1,0:T(4,128)S(1)}, f32[42,4,128]{2,1,0:T(4,128)S(1)}, u32[]{:S(2)}, u32[]{:S(2)}) collective-permute-start(f32[42,4,128]{2,1,0:T(4,128)S(1)} %get-tuple-element.40), channel_id=1, source_target_pairs={{0,2},{1,3},{2,0},{3,1},{4,6},{5,7},{6,4},{7,5},{8,10},{9,11},{10,... | collective-permute-start | bytes 258056 | tf_op jit(solution)/shard_map/ppermute | solution.py:416
  6.9 0.0 collective-permute-start.2
  7.0 0.0 copy-start.2
  7.0 0.0 copy-start.1
  7.0 0.7 %copy-done.2 = s32[128]{0:T(128)S(1)} copy-done((s32[128]{0:T(128)S(1)}, s32[128]{0:T(128)}, u32[]{:S(2)}) %copy-start.2) | copy-done | bytes 536
  7.6 0.0 collective-permute-done.refs_1_
  7.6 6.2 %collective-permute-done.1.refs_2_ = f32[42,4,128]{2,1,0:T(4,128)S(1)} collective-permute-done((f32[42,4,128]{2,1,0:T(4,128)S(1)}, f32[42,4,128]{2,1,0:T(4,128)S(1)}, u32[]{:S(2)}, u32[]{:S(2)}) %collective-permute-start.1) | collective-permute-done | bytes 86048 | tf_op jit(solution)/shard_map/ppermute | solution.py:416
  13.9 0.0 collective-permute-done.2.refs_3_
  13.9 0.0 copy-start
  13.9 0.3 shard_map.74
  14.1 2.5 %collective-permute-start.4 = (f32[32,128]{1,0:T(8,128)S(1)}, f32[32,128]{1,0:T(8,128)S(1)}, u32[]{:S(2)}, u32[]{:S(2)}) collective-permute-start(f32[32,128]{1,0:T(8,128)S(1)} %get-tuple-element.48), channel_id=1, source_target_pairs={{0,2},{1,3},{2,0},{3,1},{4,6},{5,7},{6,4},{7,5},{8,10},{9,11},{10,... | collective-permute-start | bytes 49160 | tf_op jit(solution)/shard_map/ppermute | solution.py:416
  16.7 1.4 %collective-permute-start.5 = (f32[32,128]{1,0:T(8,128)S(1)}, f32[32,128]{1,0:T(8,128)S(1)}, u32[]{:S(2)}, u32[]{:S(2)}) collective-permute-start(f32[32,128]{1,0:T(8,128)S(1)} %get-tuple-element.48), channel_id=1, source_target_pairs={{0,3},{1,2},{2,1},{3,0},{4,7},{5,6},{6,5},{7,4},{8,11},{9,10},{10,... | collective-permute-start | bytes 49160 | tf_op jit(solution)/shard_map/ppermute | solution.py:416
  18.0 0.0 collective-permute-start.3
  18.0 0.1 select_reduce_fusion
  18.1 0.0 copy-done.1
  18.2 0.3 shard_map.75
  18.5 0.4 collective-permute-done.4.refs_2_
  18.8 3.4 %collective-permute-done.5.refs_3_ = f32[32,128]{1,0:T(8,128)S(1)} collective-permute-done((f32[32,128]{1,0:T(8,128)S(1)}, f32[32,128]{1,0:T(8,128)S(1)}, u32[]{:S(2)}, u32[]{:S(2)}) %collective-permute-start.5) | collective-permute-done | bytes 16416 | tf_op jit(solution)/shard_map/ppermute | solution.py:416
  22.2 0.0 collective-permute-done.3.refs_1_
  22.2 0.0 copy-done
  22.2 0.1 shard_map.76
  22.4 0.1 collective-permute-start.6
  22.5 1.6 %collective-permute-start.8 = (f32[48,128]{1,0:T(8,128)S(1)}, f32[48,128]{1,0:T(8,128)S(1)}, u32[]{:S(2)}, u32[]{:S(2)}) collective-permute-start(f32[48,128]{1,0:T(8,128)S(1)} %get-tuple-element.56), channel_id=1, source_target_pairs={{0,16},{16,0},{1,17},{17,1},{2,18},{18,2},{3,19},{19,3},{4,20},{20... | collective-permute-start | bytes 73736 | tf_op jit(solution)/shard_map/ppermute | solution.py:465
  24.0 1.3 %collective-permute-start.7 = (f32[16,128]{1,0:T(8,128)S(1)}, f32[16,128]{1,0:T(8,128)S(1)}, u32[]{:S(2)}, u32[]{:S(2)}) collective-permute-start(f32[16,128]{1,0:T(8,128)S(1)} %slice.6), channel_id=1, source_target_pairs={{0,4},{4,0},{8,12},{12,8},{1,5},{5,1},{9,13},{13,9},{2,6},{6,2},{1... | collective-permute-start | bytes 24584 | tf_op jit(solution)/shard_map/ppermute | solution.py:467
  25.3 0.3 shard_map.77
  25.6 0.5 %collective-permute-done.7.refs_5_ = f32[16,128]{1,0:T(8,128)S(1)} collective-permute-done((f32[16,128]{1,0:T(8,128)S(1)}, f32[16,128]{1,0:T(8,128)S(1)}, u32[]{:S(2)}, u32[]{:S(2)}) %collective-permute-start.7) | collective-permute-done | bytes 8224 | tf_op jit(solution)/shard_map/ppermute | solution.py:467
  26.1 0.2 collective-permute-done.8.refs_6_
  26.4 0.0 collective-permute-done.6.refs_4_
  26.4 0.3 shard_map.78
  26.6 0.1 collective-permute-start.9
  26.7 2.7 %collective-permute-start.10 = (f32[32,128]{1,0:T(8,128)S(1)}, f32[32,128]{1,0:T(8,128)S(1)}, u32[]{:S(2)}, u32[]{:S(2)}) collective-permute-start(f32[32,128]{1,0:T(8,128)S(1)} %get-tuple-element.63), channel_id=1, source_target_pairs={{0,2},{1,3},{2,0},{3,1},{4,6},{5,7},{6,4},{7,5},{8,10},{9,11},{10,... | collective-permute-start | bytes 49160 | tf_op jit(solution)/shard_map/ppermute | solution.py:416
  29.5 1.6 %collective-permute-start.11 = (f32[32,128]{1,0:T(8,128)S(1)}, f32[32,128]{1,0:T(8,128)S(1)}, u32[]{:S(2)}, u32[]{:S(2)}) collective-permute-start(f32[32,128]{1,0:T(8,128)S(1)} %get-tuple-element.63), channel_id=1, source_target_pairs={{0,3},{1,2},{2,1},{3,0},{4,7},{5,6},{6,5},{7,4},{8,11},{9,10},{10,... | collective-permute-start | bytes 49160 | tf_op jit(solution)/shard_map/ppermute | solution.py:416
  31.1 0.3 shard_map.79
  31.4 0.0 collective-permute-done.10.refs_2_
  31.4 3.6 %collective-permute-done.11.refs_3_ = f32[32,128]{1,0:T(8,128)S(1)} collective-permute-done((f32[32,128]{1,0:T(8,128)S(1)}, f32[32,128]{1,0:T(8,128)S(1)}, u32[]{:S(2)}, u32[]{:S(2)}) %collective-permute-start.11) | collective-permute-done | bytes 16416 | tf_op jit(solution)/shard_map/ppermute | solution.py:416
  35.0 0.0 collective-permute-done.9.refs_1_
  35.0 0.1 shard_map.80
  35.1 0.1 collective-permute-start.12
  35.2 1.6 %collective-permute-start.14 = (f32[48,128]{1,0:T(8,128)S(1)}, f32[48,128]{1,0:T(8,128)S(1)}, u32[]{:S(2)}, u32[]{:S(2)}) collective-permute-start(f32[48,128]{1,0:T(8,128)S(1)} %get-tuple-element.70), channel_id=1, source_target_pairs={{0,16},{16,0},{1,17},{17,1},{2,18},{18,2},{3,19},{19,3},{4,20},{20... | collective-permute-start | bytes 73736 | tf_op jit(solution)/shard_map/ppermute | solution.py:465
  36.8 1.3 %collective-permute-start.13 = (f32[16,128]{1,0:T(8,128)S(1)}, f32[16,128]{1,0:T(8,128)S(1)}, u32[]{:S(2)}, u32[]{:S(2)}) collective-permute-start(f32[16,128]{1,0:T(8,128)S(1)} %slice.7), channel_id=1, source_target_pairs={{0,4},{4,0},{8,12},{12,8},{1,5},{5,1},{9,13},{13,9},{2,6},{6,2},{1... | collective-permute-start | bytes 24584 | tf_op jit(solution)/shard_map/ppermute | solution.py:467
  38.1 0.3 shard_map.81
  38.3 0.5 %collective-permute-done.13.refs_5_ = f32[16,128]{1,0:T(8,128)S(1)} collective-permute-done((f32[16,128]{1,0:T(8,128)S(1)}, f32[16,128]{1,0:T(8,128)S(1)}, u32[]{:S(2)}, u32[]{:S(2)}) %collective-permute-start.13) | collective-permute-done | bytes 8224 | tf_op jit(solution)/shard_map/ppermute | solution.py:467
  38.9 0.2 collective-permute-done.14.refs_6_
  39.1 0.0 collective-permute-done.12.refs_4_
  39.1 0.9 %shard_map.82 = f32[576,128]{1,0:T(8,128)} custom-call(f32[576,128]{1,0:T(8,128)S(1)} %get-tuple-element.67.refs_0_, f32[288,128]{1,0:T(8,128)S(1)} %get-tuple-element.68.refs_1_, s32[288,128]{1,0:T(8,128)S(1)} %bitcast.15, f32[1440,128]{1,0:T(8,128)S(1)} %bitcast.9, f32[64,128]{1,0:T(8,128)S(1)} %collective-permute-done.12.refs_4_, ...), custom_call_target="tpu_custom_call" | custom-call | tf_op jit(solution)/shard_map/pallas_call | solution.py:18
  (4 shorter events, 0.0 us)
Async XLA Ops:
  1.2 6.4 %collective-permute-start = (f32[42,4,128]{2,1,0:T(4,128)S(1)}, f32[42,4,128]{2,1,0:T(4,128)S(1)}, u32[]{:S(2)}, u32[]{:S(2)}) collective-permute-start(f32[42,4,128]{2,1,0:T(4,128)S(1)} %get-tuple-element.39), channel_id=1, source_target_pairs={{0,1},{1,0},{2,3},{3,2},{4,5},{5,4},{6,7},{7,6},{8,9},{9,8},{10,11... | collective-permute-start | bytes 258056 | tf_op jit(solution)/shard_map/ppermute | solution.py:416
  4.4 9.5 %collective-permute-start.1 = (f32[42,4,128]{2,1,0:T(4,128)S(1)}, f32[42,4,128]{2,1,0:T(4,128)S(1)}, u32[]{:S(2)}, u32[]{:S(2)}) collective-permute-start(f32[42,4,128]{2,1,0:T(4,128)S(1)} %get-tuple-element.40), channel_id=1, source_target_pairs={{0,2},{1,3},{2,0},{3,1},{4,6},{5,7},{6,4},{7,5},{8,10},{9,11},{10,... | collective-permute-start | bytes 258056 | tf_op jit(solution)/shard_map/ppermute | solution.py:416
  6.9 6.9 %collective-permute-start.2 = (f32[42,4,128]{2,1,0:T(4,128)S(1)}, f32[42,4,128]{2,1,0:T(4,128)S(1)}, u32[]{:S(2)}, u32[]{:S(2)}) collective-permute-start(f32[42,4,128]{2,1,0:T(4,128)S(1)} %get-tuple-element.41), channel_id=1, source_target_pairs={{0,3},{1,2},{2,1},{3,0},{4,7},{5,6},{6,5},{7,4},{8,11},{9,10},{10,... | collective-permute-start | bytes 258056 | tf_op jit(solution)/shard_map/ppermute | solution.py:416
  7.0 0.7 %copy-start.2 = (s32[128]{0:T(128)S(1)}, s32[128]{0:T(128)}, u32[]{:S(2)}) copy-start(s32[128]{0:T(128)} %param.13) | copy-start | bytes 1540
  7.0 11.2 %copy-start.1 = (s32[18,16,128]{2,1,0:T(8,128)S(1)}, s32[18,16,128]{2,1,0:T(8,128)}, u32[]{:S(2)}) copy-start(s32[18,16,128]{2,1,0:T(8,128)} %param.9) | copy-start | bytes 442372
  13.9 8.4 %copy-start = (f32[5,18,16,128]{3,2,1,0:T(8,128)S(1)}, f32[5,18,16,128]{3,2,1,0:T(8,128)}, u32[]{:S(2)}) copy-start(f32[5,18,16,128]{3,2,1,0:T(8,128)} %param.8) | copy-start | bytes 2211844
  14.1 4.7 %collective-permute-start.4 = (f32[32,128]{1,0:T(8,128)S(1)}, f32[32,128]{1,0:T(8,128)S(1)}, u32[]{:S(2)}, u32[]{:S(2)}) collective-permute-start(f32[32,128]{1,0:T(8,128)S(1)} %get-tuple-element.48), channel_id=1, source_target_pairs={{0,2},{1,3},{2,0},{3,1},{4,6},{5,7},{6,4},{7,5},{8,10},{9,11},{10,... | collective-permute-start | bytes 49160 | tf_op jit(solution)/shard_map/ppermute | solution.py:416
  16.7 5.5 %collective-permute-start.5 = (f32[32,128]{1,0:T(8,128)S(1)}, f32[32,128]{1,0:T(8,128)S(1)}, u32[]{:S(2)}, u32[]{:S(2)}) collective-permute-start(f32[32,128]{1,0:T(8,128)S(1)} %get-tuple-element.48), channel_id=1, source_target_pairs={{0,3},{1,2},{2,1},{3,0},{4,7},{5,6},{6,5},{7,4},{8,11},{9,10},{10,... | collective-permute-start | bytes 49160 | tf_op jit(solution)/shard_map/ppermute | solution.py:416
  18.0 4.2 %collective-permute-start.3 = (f32[64,128]{1,0:T(8,128)S(1)}, f32[64,128]{1,0:T(8,128)S(1)}, u32[]{:S(2)}, u32[]{:S(2)}) collective-permute-start(f32[64,128]{1,0:T(8,128)S(1)} %get-tuple-element.47.refs_0_), channel_id=1, source_target_pairs={{0,1},{1,0},{2,3},{3,2},{4,5},{5,4},{6,7},{7,6},{8,9},{9,8},{10,11... | collective-permute-start | bytes 98312 | tf_op jit(solution)/shard_map/ppermute | solution.py:416
  22.4 4.0 %collective-permute-start.6 = (f32[64,128]{1,0:T(8,128)S(1)}, f32[64,128]{1,0:T(8,128)S(1)}, u32[]{:S(2)}, u32[]{:S(2)}) collective-permute-start(f32[64,128]{1,0:T(8,128)S(1)} %get-tuple-element.55), channel_id=1, source_target_pairs={{0,12},{4,8},{8,4},{12,0},{1,13},{5,9},{9,5},{13,1},{2,14},{6,10},... | collective-permute-start | bytes 98312 | tf_op jit(solution)/shard_map/ppermute | solution.py:466
  22.5 3.9 %collective-permute-start.8 = (f32[48,128]{1,0:T(8,128)S(1)}, f32[48,128]{1,0:T(8,128)S(1)}, u32[]{:S(2)}, u32[]{:S(2)}) collective-permute-start(f32[48,128]{1,0:T(8,128)S(1)} %get-tuple-element.56), channel_id=1, source_target_pairs={{0,16},{16,0},{1,17},{17,1},{2,18},{18,2},{3,19},{19,3},{4,20},{20... | collective-permute-start | bytes 73736 | tf_op jit(solution)/shard_map/ppermute | solution.py:465
  24.0 2.1 %collective-permute-start.7 = (f32[16,128]{1,0:T(8,128)S(1)}, f32[16,128]{1,0:T(8,128)S(1)}, u32[]{:S(2)}, u32[]{:S(2)}) collective-permute-start(f32[16,128]{1,0:T(8,128)S(1)} %slice.6), channel_id=1, source_target_pairs={{0,4},{4,0},{8,12},{12,8},{1,5},{5,1},{9,13},{13,9},{2,6},{6,2},{1... | collective-permute-start | bytes 24584 | tf_op jit(solution)/shard_map/ppermute | solution.py:467
  26.6 8.4 %collective-permute-start.9 = (f32[64,128]{1,0:T(8,128)S(1)}, f32[64,128]{1,0:T(8,128)S(1)}, u32[]{:S(2)}, u32[]{:S(2)}) collective-permute-start(f32[64,128]{1,0:T(8,128)S(1)} %get-tuple-element.62.refs_0_), channel_id=1, source_target_pairs={{0,1},{1,0},{2,3},{3,2},{4,5},{5,4},{6,7},{7,6},{8,9},{9,8},{10,11... | collective-permute-start | bytes 98312 | tf_op jit(solution)/shard_map/ppermute | solution.py:416
  26.7 4.7 %collective-permute-start.10 = (f32[32,128]{1,0:T(8,128)S(1)}, f32[32,128]{1,0:T(8,128)S(1)}, u32[]{:S(2)}, u32[]{:S(2)}) collective-permute-start(f32[32,128]{1,0:T(8,128)S(1)} %get-tuple-element.63), channel_id=1, source_target_pairs={{0,2},{1,3},{2,0},{3,1},{4,6},{5,7},{6,4},{7,5},{8,10},{9,11},{10,... | collective-permute-start | bytes 49160 | tf_op jit(solution)/shard_map/ppermute | solution.py:416
  29.5 5.5 %collective-permute-start.11 = (f32[32,128]{1,0:T(8,128)S(1)}, f32[32,128]{1,0:T(8,128)S(1)}, u32[]{:S(2)}, u32[]{:S(2)}) collective-permute-start(f32[32,128]{1,0:T(8,128)S(1)} %get-tuple-element.63), channel_id=1, source_target_pairs={{0,3},{1,2},{2,1},{3,0},{4,7},{5,6},{6,5},{7,4},{8,11},{9,10},{10,... | collective-permute-start | bytes 49160 | tf_op jit(solution)/shard_map/ppermute | solution.py:416
  35.1 4.0 %collective-permute-start.12 = (f32[64,128]{1,0:T(8,128)S(1)}, f32[64,128]{1,0:T(8,128)S(1)}, u32[]{:S(2)}, u32[]{:S(2)}) collective-permute-start(f32[64,128]{1,0:T(8,128)S(1)} %get-tuple-element.69), channel_id=1, source_target_pairs={{0,12},{4,8},{8,4},{12,0},{1,13},{5,9},{9,5},{13,1},{2,14},{6,10},... | collective-permute-start | bytes 98312 | tf_op jit(solution)/shard_map/ppermute | solution.py:466
  35.2 3.9 %collective-permute-start.14 = (f32[48,128]{1,0:T(8,128)S(1)}, f32[48,128]{1,0:T(8,128)S(1)}, u32[]{:S(2)}, u32[]{:S(2)}) collective-permute-start(f32[48,128]{1,0:T(8,128)S(1)} %get-tuple-element.70), channel_id=1, source_target_pairs={{0,16},{16,0},{1,17},{17,1},{2,18},{18,2},{3,19},{19,3},{4,20},{20... | collective-permute-start | bytes 73736 | tf_op jit(solution)/shard_map/ppermute | solution.py:465
  36.8 2.1 %collective-permute-start.13 = (f32[16,128]{1,0:T(8,128)S(1)}, f32[16,128]{1,0:T(8,128)S(1)}, u32[]{:S(2)}, u32[]{:S(2)}) collective-permute-start(f32[16,128]{1,0:T(8,128)S(1)} %slice.7), channel_id=1, source_target_pairs={{0,4},{4,0},{8,12},{12,8},{1,5},{5,1},{9,13},{13,9},{2,6},{6,2},{1... | collective-permute-start | bytes 24584 | tf_op jit(solution)/shard_map/ppermute | solution.py:467
